TPU v7x, 32 devices: a whole 2x2x4 slice. The times are simulated.
32 devices in a mesh: pipe: 4 (over x, core), dp: 8 (over z, y).
Axes of the slice: x: 2, y: 2, z: 4, core: 2. Of those that a mesh axis runs over, the one named last changes fastest.
Arguments:
- section_input: bfloat16 [4, 2048, 2048], P('pipe', 'dp'), may hold values from -6 to 6
- top_grad: bfloat16 [2048, 2048], P('dp'), may hold values from -6 to 6
- w_in: bfloat16 [4, 2048, 3072], P('pipe', 'dp'), may hold values from -0.125 to 0.125
- w_out: bfloat16 [4, 1024, 2048], P('pipe', 'dp'), may hold values from -0.1875 to 0.1875
- segments: int32 [16, 128], P('dp'), may hold values from 0 to 3, never falling along the last dimension, each value on 1 to 64 neighbouring positions
Outputs:
- section_grads: bfloat16 [4, 2048, 2048], P('pipe', 'dp')
- w_in_grad: float32 [4, 2048, 3072], P('pipe', 'dp')
- w_out_grad: float32 [4, 1024, 2048], P('pipe', 'dp')
Inputs may be any that keep to these rules, and one draw needn't show every extreme that they name: `segments`: in every row the history numbers run 0 to 3 without falling, each history has 1 to 64 positions, and one has exactly 64.
All inputs are finite; a program needn't handle non-finite values.
Results may differ from a plain program's by a relative error of at most 0.03.
Values may be sent and summed in bfloat16 or wider, within the bound.
A program may use at most 128 MiB of HBM per device.

v0:
```python
import functools

import jax
import jax.numpy as jnp
from jax import lax
from jax.experimental import pallas as pl
from jax.experimental.pallas import tpu as pltpu
from jax.sharding import PartitionSpec as P

HEADS = 16
QK_DIM = 32
V_DIM = 64
LANES = 128

EPSILON = 1e-05
MESH = pl.DeviceIdType.MESH
VMEM = pl.BlockSpec(memory_space=pltpu.VMEM)

QK_HEADS = LANES // QK_DIM
V_HEADS = LANES // V_DIM
GROUPS = HEADS // QK_HEADS
V_COLS = HEADS * V_DIM
Q_COLS = HEADS * QK_DIM
GROUP_V = QK_HEADS * V_DIM
SCALE = QK_DIM ** (-0.5)


def norm_rows(values):
    center = values - jnp.mean(values, axis=-1, keepdims=True)
    return center * lax.rsqrt(jnp.mean(center * center, axis=-1, keepdims=True) + EPSILON)


def silu_slope(preact):
    squash = jax.nn.sigmoid(preact)
    return squash * (1.0 + preact * (1.0 - squash))


def dot_nt(left, right):
    return lax.dot_general(
        left, right, (((1,), (1,)), ((), ())), preferred_element_type=jnp.float32
    )


def dot_nn(left, right):
    return lax.dot_general(
        left, right, (((1,), (0,)), ((), ())), preferred_element_type=jnp.float32
    )


def contract_rows(left, right):
    return lax.dot_general(
        left, right, (((0,), (0,)), ((), ())), preferred_element_type=jnp.float32
    )


def only_head(block, lane, width, index):
    keep = jnp.logical_and(lane >= index * width, lane < (index + 1) * width)
    return jnp.where(keep, block, jnp.zeros_like(block))


def at(start, size):
    return pl.ds(pl.multiple_of(start, LANES), size)


def attend_kernel(micro, length, act_ref, mask_ref, score_ref, unit_ref, rstd_ref, gated_ref, mixed):
    lane = lax.broadcasted_iota(jnp.int32, (length, LANES), 1)

    def one(index, _):
        slot, group = index // GROUPS, index % GROUPS
        rows = at(slot * length, length)
        queries = act_ref[rows, at(2 * V_COLS + group * LANES, LANES)]
        keys = act_ref[rows, at(2 * V_COLS + Q_COLS + group * LANES, LANES)]
        mask = mask_ref[rows, :]
        for half in range(GROUP_V // LANES):
            cols = group * GROUP_V + half * LANES
            values = act_ref[rows, at(V_COLS + cols, LANES)]
            total = jnp.zeros((length, LANES), jnp.float32)
            for sub in range(V_HEADS):
                head = half * V_HEADS + sub
                score = dot_nt(only_head(queries, lane, QK_DIM, head), keys) * SCALE
                score_ref[at((index * QK_HEADS + head) * length, length), :] = score
                weight = (jax.nn.silu(score) * mask).astype(jnp.bfloat16)
                total += dot_nn(weight, only_head(values, lane, V_DIM, sub))
            mixed[rows, at(cols, LANES)] = total
        return 0

    lax.fori_loop(0, micro * GROUPS, one, 0)

    def finish(slot, _):
        rows = at(slot * length, length)
        value = mixed[rows, :]
        center = value - jnp.mean(value, axis=-1, keepdims=True)
        rstd = lax.rsqrt(jnp.mean(center * center, axis=-1, keepdims=True) + EPSILON)
        unit = center * rstd
        unit_ref[rows, :] = unit
        rstd_ref[rows, :] = jnp.broadcast_to(rstd, (length, LANES))
        gated_ref[rows, :] = (unit * act_ref[rows, :V_COLS].astype(jnp.float32)).astype(jnp.bfloat16)
        return 0

    lax.fori_loop(0, micro, finish, 0)


def attend(activated, mask, micro, length):
    tokens = micro * length
    return pl.pallas_call(
        functools.partial(attend_kernel, micro, length),
        out_shape=(
            jax.ShapeDtypeStruct((micro * HEADS * length, length), jnp.float32),
            jax.ShapeDtypeStruct((tokens, V_COLS), jnp.float32),
            jax.ShapeDtypeStruct((tokens, LANES), jnp.float32),
            jax.ShapeDtypeStruct((tokens, V_COLS), jnp.bfloat16),
        ),
        in_specs=[VMEM] * 2,
        out_specs=(VMEM,) * 4,
        scratch_shapes=[pltpu.VMEM((tokens, V_COLS), jnp.float32)],
        name="attend",
    )(activated, mask)


def chain_kernel(
    micro, length, sections,
    top_ref, input_ref, act_ref, pre_ref, score_ref, unit_ref, rstd_ref, mask_ref, first_ref, second_ref,
    up_ref, gpre_ref, gin_ref,
    landed, leaving, ggate, dmix, gnorm, send_sem, recv_sem,
):
    section = lax.axis_index("pipe")
    width = input_ref.shape[1]
    tile = 2 * LANES
    lane = lax.broadcasted_iota(jnp.int32, (length, LANES), 1)
    is_last = section == sections - 1
    is_first = section == 0

    barrier = pltpu.get_barrier_semaphore()

    @pl.when(jnp.logical_not(is_last))
    def _():
        pl.semaphore_signal(
            barrier, inc=1, device_id={"pipe": jnp.minimum(section + 1, sections - 1)}, device_id_type=MESH
        )

    @pl.when(jnp.logical_not(is_first))
    def _():
        pl.semaphore_wait(barrier, 1)

    def copy_of(slot):
        return pltpu.make_async_remote_copy(
            src_ref=leaving.at[slot],
            dst_ref=landed.at[slot],
            send_sem=send_sem.at[slot],
            recv_sem=recv_sem.at[slot],
            device_id={"pipe": jnp.maximum(section - 1, 0)},
            device_id_type=MESH,
        )

    def store_grad(rows, cols, size, value):
        rounded = value.astype(jnp.bfloat16).astype(jnp.float32)
        gpre_ref[rows, at(cols, size)] = (
            rounded * silu_slope(pre_ref[rows, at(cols, size)])
        ).astype(jnp.bfloat16)

    for slot in range(micro):
        rows = pl.ds(slot * length, length)

        @pl.when(is_last)
        def _():
            up_ref[rows, :] = top_ref[rows, :]

        @pl.when(jnp.logical_not(is_last))
        def _():
            copy_of(slot).wait_recv()
            up_ref[rows, :] = landed[slot]

        def gate_tile(index, _):
            ggate[:, at(index * tile, tile)] = dot_nt(up_ref[rows, :], second_ref[at(index * tile, tile), :])
            return 0

        lax.fori_loop(0, V_COLS // tile, gate_tile, 0)
        gating = act_ref[rows, :V_COLS].astype(jnp.float32)
        unit = unit_ref[rows, :]
        grad = ggate[...]
        store_grad(rows, 0, V_COLS, grad * unit)
        grad = grad * gating
        mean_grad = jnp.mean(grad, axis=-1, keepdims=True)
        mean_unit = jnp.mean(grad * unit, axis=-1, keepdims=True)
        dmix[...] = (rstd_ref[rows, :1] * (grad - mean_grad - unit * mean_unit)).astype(jnp.bfloat16)

        def one(group, _):
            queries = act_ref[rows, at(2 * V_COLS + group * LANES, LANES)]
            keys = act_ref[rows, at(2 * V_COLS + Q_COLS + group * LANES, LANES)]
            mask = mask_ref[rows, :]
            grad_q = jnp.zeros((length, LANES), jnp.float32)
            grad_k = jnp.zeros((length, LANES), jnp.float32)
            for half in range(GROUP_V // LANES):
                cols = group * GROUP_V + half * LANES
                values = act_ref[rows, at(V_COLS + cols, LANES)]
                grad_mix = dmix[:, at(cols, LANES)]
                grad_v = jnp.zeros((length, LANES), jnp.float32)
                for sub in range(V_HEADS):
                    head = half * V_HEADS + sub
                    mix_head = only_head(grad_mix, lane, V_DIM, sub)
                    place = (slot * HEADS + group * QK_HEADS + head) * length
                    score = score_ref[at(place, length), :]
                    squash = jax.nn.sigmoid(score)
                    weight = (score * squash * mask).astype(jnp.bfloat16)
                    slope = squash * (1.0 + score * (1.0 - squash)) * mask * SCALE
                    grad_score = (dot_nt(mix_head, values) * slope).astype(jnp.bfloat16)
                    grad_v += contract_rows(weight, mix_head)
                    grad_q += dot_nn(grad_score, only_head(keys, lane, QK_DIM, head))
                    grad_k += contract_rows(grad_score, only_head(queries, lane, QK_DIM, head))
                store_grad(rows, V_COLS + cols, LANES, grad_v)
            store_grad(rows, 2 * V_COLS + group * LANES, LANES, grad_q)
            store_grad(rows, 2 * V_COLS + Q_COLS + group * LANES, LANES, grad_k)
            return 0

        lax.fori_loop(0, GROUPS, one, 0)

        def norm_tile(index, _):
            gnorm[:, at(index * tile, tile)] = dot_nt(gpre_ref[rows, :], first_ref[at(index * tile, tile), :])
            return 0

        lax.fori_loop(0, width // tile, norm_tile, 0)
        value = input_ref[rows, :].astype(jnp.float32)
        center = value - jnp.mean(value, axis=-1, keepdims=True)
        rstd = lax.rsqrt(jnp.mean(center * center, axis=-1, keepdims=True) + EPSILON)
        unit = center * rstd
        grad = gnorm[...]
        mean_grad = jnp.mean(grad, axis=-1, keepdims=True)
        mean_unit = jnp.mean(grad * unit, axis=-1, keepdims=True)
        through = rstd * (grad - mean_grad - unit * mean_unit)
        result = (up_ref[rows, :].astype(jnp.float32) + through).astype(jnp.bfloat16)
        leaving[slot] = result
        gin_ref[rows, :] = result

        @pl.when(jnp.logical_not(is_first))
        def _():
            copy_of(slot).start()

    for slot in range(micro):

        @pl.when(jnp.logical_not(is_first))
        def _():
            copy_of(slot).wait_send()


def chain(top, inputs, activated, preact, scores, unit, rstd, mask, w_first, w_second, micro, length):
    tokens, width = inputs.shape
    return pl.pallas_call(
        functools.partial(chain_kernel, micro, length, lax.axis_size("pipe")),
        out_shape=(
            jax.ShapeDtypeStruct((tokens, width), jnp.bfloat16),
            jax.ShapeDtypeStruct(preact.shape, jnp.bfloat16),
            jax.ShapeDtypeStruct((tokens, width), jnp.bfloat16),
        ),
        in_specs=[VMEM] * 10,
        out_specs=(VMEM,) * 3,
        scratch_shapes=[
            pltpu.VMEM((micro, length, width), jnp.bfloat16),
            pltpu.VMEM((micro, length, width), jnp.bfloat16),
            pltpu.VMEM((length, V_COLS), jnp.float32),
            pltpu.VMEM((length, V_COLS), jnp.bfloat16),
            pltpu.VMEM((length, width), jnp.float32),
            pltpu.SemaphoreType.DMA((micro,)),
            pltpu.SemaphoreType.DMA((micro,)),
        ],
        compiler_params=pltpu.CompilerParams(
            collective_id=0, has_side_effects=True, vmem_limit_bytes=60 * 1024 * 1024
        ),
        name="chain",
    )(top, inputs, activated, preact, scores, unit, rstd, mask, w_first, w_second)


def add_into(target, left, right):
    step = 32

    def one(index, _):
        rows = pl.ds(pl.multiple_of(index * step, step), step)
        total = left[rows, :].astype(jnp.float32) + right[rows, :].astype(jnp.float32)
        target[rows, :] = total.astype(target.dtype)
        return 0

    lax.fori_loop(0, target.shape[0] // step, one, 0)


def scatter_kernel(line, part_a, part_b, out_a, out_b, *scratch):
    pairs = (
        (part_a, out_a) + scratch[0:4],
        (part_b, out_b) + scratch[4:8],
    )
    load_sem, pair_send, pair_recv, right_send, right_recv, left_send, left_recv = scratch[8:]
    rank = lax.axis_index("dp")
    spot, lane_of = rank // 2, rank % 2
    has_left, has_right = spot > 0, spot < line - 1
    partner = spot * 2 + 1 - lane_of
    right = jnp.minimum(spot + 1, line - 1) * 2 + lane_of
    left = jnp.maximum(spot - 1, 0) * 2 + lane_of

    barrier = pltpu.get_barrier_semaphore()
    pl.semaphore_signal(barrier, inc=1, device_id={"dp": partner}, device_id_type=MESH)

    @pl.when(has_left)
    def _():
        pl.semaphore_signal(barrier, inc=1, device_id={"dp": left}, device_id_type=MESH)

    @pl.when(has_right)
    def _():
        pl.semaphore_signal(barrier, inc=1, device_id={"dp": right}, device_id_type=MESH)

    pl.semaphore_wait(barrier, 1 + jnp.minimum(spot, 1) + jnp.minimum(line - 1 - spot, 1))

    def block_at(turn):
        near = jnp.minimum(spot, line - 1 - spot)
        ahead = line - 1 - 2 * near
        lone = jnp.where(spot <= line - 1 - spot, line - 1 - turn, turn)
        after = jnp.maximum(turn - ahead, 0)
        reach = near - after // 2
        both = jnp.where(after % 2 == 0, spot + reach, spot - reach)
        return jnp.where(turn < ahead, lone, both)

    def load_of(which, block):
        part, _, own, _, _, _ = pairs[which]
        return pltpu.make_async_copy(part.at[block, lane_of], own.at[block], load_sem.at[which, block])

    def pair_of(which, block):
        part, _, _, paired, _, _ = pairs[which]
        return pltpu.make_async_remote_copy(
            src_ref=part.at[block, 1 - lane_of], dst_ref=paired.at[block],
            send_sem=pair_send.at[which, block], recv_sem=pair_recv.at[which, block],
            device_id={"dp": partner}, device_id_type=MESH,
        )

    def flow_of(which, block, rightward, source):
        flow = pairs[which][4 if rightward else 5]
        sends, recvs = (right_send, right_recv) if rightward else (left_send, left_recv)
        return pltpu.make_async_remote_copy(
            src_ref=source.at[block], dst_ref=flow.at[block],
            send_sem=sends.at[which, block], recv_sem=recvs.at[which, block],
            device_id={"dp": right if rightward else left}, device_id_type=MESH,
        )

    def begin(turn, _):
        block = block_at(turn)
        for which in range(2):
            pair_of(which, block).start()
            load_of(which, block).start()
        return 0

    lax.fori_loop(0, line, begin, 0)

    def pass_on(turn, _):
        block = block_at(turn)
        for which in range(2):
            own, paired = pairs[which][2:4]
            load_of(which, block).wait()
            pair_of(which, block).wait_recv()
            add_into(own.at[block], own.at[block], paired.at[block])
            for rightward in (True, False):
                flow = pairs[which][4 if rightward else 5]
                fed = has_left if rightward else has_right
                wanted = block > spot if rightward else block < spot

                @pl.when(jnp.logical_and(wanted, fed))
                def _():
                    flow_of(which, block, rightward, flow).wait_recv()
                    add_into(flow.at[block], flow.at[block], own.at[block])
                    flow_of(which, block, rightward, flow).start()

                @pl.when(jnp.logical_and(wanted, jnp.logical_not(fed)))
                def _():
                    flow_of(which, block, rightward, own).start()
        return 0

    lax.fori_loop(0, line, pass_on, 0)

    for which in range(2):
        out, own = pairs[which][1:3]
        for rightward in (True, False):
            flow = pairs[which][4 if rightward else 5]

            @pl.when(has_left if rightward else has_right)
            def _():
                flow_of(which, spot, rightward, flow).wait_recv()

        @pl.when(jnp.logical_and(has_left, has_right))
        def _():
            add_into(out, own.at[spot], pairs[which][4].at[spot])
            add_into(out, out, pairs[which][5].at[spot])

        @pl.when(jnp.logical_and(has_left, jnp.logical_not(has_right)))
        def _():
            add_into(out, own.at[spot], pairs[which][4].at[spot])

        @pl.when(jnp.logical_and(has_right, jnp.logical_not(has_left)))
        def _():
            add_into(out, own.at[spot], pairs[which][5].at[spot])

    def finish(block, _):
        for which in range(2):
            pair_of(which, block).wait_send()
            for rightward in (True, False):

                @pl.when(block > spot if rightward else block < spot)
                def _():
                    flow_of(which, block, rightward, pairs[which][2]).wait_send()
        return 0

    lax.fori_loop(0, line, finish, 0)


def scatter_sums(part_a, part_b):
    devices = lax.axis_size("dp")
    line = devices // 2
    parts = [part.reshape(line, 2, part.shape[0] // devices, part.shape[1]) for part in (part_a, part_b)]
    scratch = []
    for part in parts:
        scratch += [pltpu.VMEM((line,) + part.shape[2:], part.dtype)] * 4
    scratch += [pltpu.SemaphoreType.DMA((2, line))] * 7
    return pl.pallas_call(
        functools.partial(scatter_kernel, line),
        out_shape=tuple(jax.ShapeDtypeStruct(part.shape[2:], jnp.float32) for part in parts),
        in_specs=[pl.BlockSpec(memory_space=pl.ANY)] * 2,
        out_specs=(VMEM,) * 2,
        scratch_shapes=scratch,
        compiler_params=pltpu.CompilerParams(
            collective_id=1, has_side_effects=True, vmem_limit_bytes=60 * 1024 * 1024
        ),
        name="scatter_sums",
    )(*parts)


def mask_of(segments):
    length = segments.shape[1]
    same = segments[:, :, None] == segments[:, None, :]
    positions = lax.broadcasted_iota(jnp.int32, (length, length), 0)
    columns = lax.broadcasted_iota(jnp.int32, (length, length), 1)
    counts = jnp.sum(same.astype(jnp.float32), axis=2, keepdims=True)
    allowed = jnp.logical_and(same, (columns <= positions)[None])
    return (allowed.astype(jnp.float32) / counts).reshape(-1, length)


def body(section_input, top_grad, w_in, w_out, segments):
    micro, length = segments.shape
    inputs = section_input[0]
    w_first = lax.all_gather(w_in[0], "dp", axis=0, tiled=True)
    w_mine, w_first = lax.optimization_barrier((w_out[0], w_first))
    w_second = lax.all_gather(w_mine, "dp", axis=0, tiled=True)
    mask = mask_of(segments)
    normed = norm_rows(inputs.astype(jnp.float32)).astype(jnp.bfloat16)
    preact = jnp.dot(normed, w_first, preferred_element_type=jnp.float32)
    activated = jax.nn.silu(preact).astype(jnp.bfloat16)
    scores, unit, rstd, gated = attend(activated, mask, micro, length)
    upstream, grad_preact, grads = chain(
        top_grad, inputs, activated, preact, scores, unit, rstd, mask, w_first, w_second, micro, length
    )
    part_out = contract_rows(gated, upstream).astype(jnp.bfloat16)
    part_in = contract_rows(normed, grad_preact).astype(jnp.bfloat16)
    grad_first, grad_out = scatter_sums(part_in, part_out)
    return (grads[None], grad_first[None], grad_out[None])


def solution(mesh):
    return jax.shard_map(
        body,
        mesh=mesh,
        in_specs=(
            P("pipe", "dp", None),
            P("dp", None),
            P("pipe", "dp", None),
            P("pipe", "dp", None),
            P("dp", None),
        ),
        out_specs=(P("pipe", "dp", None), P("pipe", "dp", None), P("pipe", "dp", None)),
        check_vma=False,
    )
```

profile of v0, /device:TPU:4, one launch (start us, length us, event | category | flops | bytes accessed | tf_op | source)
XLA Modules:
  0.0 538.0 jit_solution(2776009500681768297)
XLA Ops:
  7.2 0.0 copy-start.6
  7.2 0.0 copy-start
  7.2 0.0 all-gather.6.cloned.1.call-start
  7.2 0.7 all-gather.6.cloned.1.call-update
  7.9 0.0 all-gather.4.cloned.1.call-start
  8.0 179.0 %all-gather.6.cloned.1.call-done = bf16[1,2048,3072]{2,1,0:T(8,128)(2,1)} async-done(((bf16[1,256,3072]{2,1,0:T(8,128)(2,1)}), bf16[1,2048,3072]{2,1,0:T(8,128)(2,1)}) %all-gather.6.cloned.1.call-update) | async-done | bytes 12582928 | tf_op jit(solution)/shard_map/all_gather | solution.py:443
  187.0 0.0 all-gather.4.cloned.1.call-update
  187.0 0.0 copy-done.6
  187.0 0.2 convert_reduce_fusion.1
  187.2 0.8 convert_divide_fusion.mask_ref
  188.0 0.0 copy-done
  188.0 0.2 convert_reduce_fusion
  188.2 0.4 fusion.2
  188.7 10.2 %multiply_convert_fusion = (bf16[256,3072]{1,0:T(8,128)(2,1)}, f32[256,3072]{1,0:T(8,128)}) fusion(bf16[2048,3072]{1,0:T(8,128)(2,1)} %bitcast.32, f32[256]{0:T(256)S(1)} %add_rsqrt_fusion, f32[256]{0:T(256)S(1)} %broadcast_multiply_fusion, bf16[1,256,2048]{2,1,0:T(8,128)(2,1)S(1)} %copy-done), kind=kOutput, calls=%fused_computation.2 | convolution fusion | flops 3227254784 | bytes 18352128 | tf_op jit(solution)/shard_map/dot_general | solution.py:448
  198.9 7.7 %attend.1 = (f32[4096,128]{1,0:T(8,128)}, f32[256,1024]{1,0:T(8,128)}, f32[256,128]{1,0:T(8,128)}, bf16[256,1024]{1,0:T(8,128)(2,1)}) custom-call(bf16[256,3072]{1,0:T(8,128)(2,1)} %get-tuple-element.25.act_ref, f32[256,128]{1,0:T(8,128)} %convert_divide_fusion.mask_ref), custom_call_target="tpu_custom_call" | custom-call | tf_op jit(solution)/shard_map/attend/pallas_call | solution.py:105
  206.5 54.2 %all-gather.4.cloned.1.call-done.second_ref = bf16[1024,2048]{1,0:T(8,128)(2,1)} async-done(((bf16[128,2048]{1,0:T(8,128)(2,1)}), bf16[1024,2048]{1,0:T(8,128)(2,1)}) %all-gather.4.cloned.1.call-update) | async-done | bytes 4194320 | tf_op jit(solution)/shard_map/all_gather | solution.py:445
  260.7 0.0 copy-start.1
  260.7 78.0 %chain.1 = (bf16[256,2048]{1,0:T(8,128)(2,1)}, bf16[256,3072]{1,0:T(8,128)(2,1)}, bf16[256,2048]{1,0:T(8,128)(2,1)}) custom-call(bf16[256,2048]{1,0:T(8,128)(2,1)} %top_ref.1, bf16[256,2048]{1,0:T(8,128)(2,1)} %bitcast.31, bf16[256,3072]{1,0:T(8,128)(2,1)} %get-tuple-element.25.act_ref, f32[256,3072]{1,0:T(8,128)} %get-tuple-element.26.pre_ref, ...), custom_call_target="tpu_custom_call" | custom-call | tf_op jit(solution)/shard_map/chain/pallas_call | solution.py:247
  338.7 0.0 copy-done.1
  338.8 0.0 copy-start.2
  338.8 0.0 copy-start.5
  338.8 8.1 %convolution_convert_fusion = bf16[2048,3072]{1,0:T(8,128)(2,1)} fusion(bf16[256,3072]{1,0:T(8,128)(2,1)} %get-tuple-element.20, f32[256]{0:T(256)S(1)} %add_rsqrt_fusion, f32[256]{0:T(256)S(1)} %broadcast_multiply_fusion, bf16[1,256,2048]{2,1,0:T(8,128)(2,1)S(1)} %copy-done.1), kind=kOutput, calls=%fused_computation | convolution fusion | flops 3229614080 | bytes 15206400 | tf_op jit(solution)/shard_map/dot_general | solution.py:51
  346.9 0.0 copy-done.2
  346.9 0.0 copy-done.5
  346.9 3.2 convolution_convert_fusion.1
  350.1 0.0 copy-start.3
  350.1 175.1 %scatter_sums.1 = (f32[256,3072]{1,0:T(8,128)}, f32[128,2048]{1,0:T(8,128)}) custom-call(bf16[4,2,256,3072]{3,2,1,0:T(8,128)(2,1)} %bitcast.29, bf16[4,2,128,2048]{3,2,1,0:T(8,128)(2,1)} %bitcast.30), custom_call_target="tpu_custom_call" | custom-call | tf_op jit(solution)/shard_map/scatter_sums/pallas_call | solution.py:417
  525.2 0.0 copy-done.3
  525.2 1.0 copy.11
  526.2 4.0 copy.12
  530.2 0.0 copy-done.4
  530.2 1.0 copy.13
  (4 shorter events, 0.0 us)
Async XLA Ops:
  7.2 179.8 %copy-start.6 = (s32[2,128]{1,0:T(2,128)S(1)}, s32[2,128]{1,0:T(2,128)}, u32[]{:S(2)}) copy-start(s32[2,128]{1,0:T(2,128)} %param.9) | copy-start | bytes 3076
  7.2 180.8 %copy-start = (bf16[1,256,2048]{2,1,0:T(8,128)(2,1)S(1)}, bf16[1,256,2048]{2,1,0:T(8,128)(2,1)}, u32[]{:S(2)}) copy-start(bf16[1,256,2048]{2,1,0:T(8,128)(2,1)} %param.5) | copy-start | bytes 3145732
  7.2 179.8 %all-gather.6.cloned.1.call-start = ((), (), s32[]{:S(2)}) async-start(), calls=%async_computation.1 | async-start | bytes 14155776 | tf_op jit(solution)/shard_map/all_gather | solution.py:443
  7.9 252.8 %all-gather.4.cloned.1.call-start = ((), (), s32[]{:S(2)}) async-start(), calls=%async_computation | async-start | bytes 4718592 | tf_op jit(solution)/shard_map/all_gather | solution.py:445
  260.7 78.0 %copy-start.1 = (bf16[1,256,2048]{2,1,0:T(8,128)(2,1)S(1)}, bf16[1,256,2048]{2,1,0:T(8,128)(2,1)}, u32[]{:S(2)}) copy-start(bf16[1,256,2048]{2,1,0:T(8,128)(2,1)} %param.5) | copy-start | bytes 3145732
  338.8 8.1 %copy-start.2 = (bf16[256,1024]{1,0:T(8,128)(2,1)S(1)}, bf16[256,1024]{1,0:T(8,128)(2,1)}, u32[]{:S(2)}) copy-start(bf16[256,1024]{1,0:T(8,128)(2,1)} %get-tuple-element.21) | copy-start | bytes 1572868
  338.8 8.1 %copy-start.5 = (bf16[256,2048]{1,0:T(8,128)(2,1)S(1)}, bf16[256,2048]{1,0:T(8,128)(2,1)}, u32[]{:S(2)}) copy-start(bf16[256,2048]{1,0:T(8,128)(2,1)} %get-tuple-element.22) | copy-start | bytes 3145732
  350.1 175.1 %copy-start.3 = (bf16[256,2048]{1,0:T(8,128)(2,1)S(1)}, bf16[256,2048]{1,0:T(8,128)(2,1)}, u32[]{:S(2)}) copy-start(bf16[256,2048]{1,0:T(8,128)(2,1)} %get-tuple-element.19) | copy-start | bytes 3145732
  526.2 4.0 copy-start.4
Sparse Core Ops, SparseCore 0:
  10.2 176.7 all-gather.5
  189.1 71.5 all-gather.3
where the time goes:
time: 540 us; the launch traced here: 538 us
  Pallas kernels  261 us (48%)
  waiting for transfers between devices  234 us (43%)
  matrix products  21.5 us (4%)
  between operations  14.1 us (3%)
  local copies, waits for them, and re-layouts  5.96 us (1%)
    all_gather x1, waiting for transfers between devices, body(): w_first = lax.all_gather(w_in[0], 'dp', axis=0, tiled=True)  179 us
    pallas_call x1, Pallas kernels, scatter_sums(): pl.pallas_call(functools.partial(scatter_kernel, line), out_shape=tuple((...  175 us
    pallas_call x1, Pallas kernels, chain(): pl.pallas_call(functools.partial(chain_kernel, micro, length, lax.axis_si...  78 us
    all_gather x1, waiting for transfers between devices, body(): w_second = lax.all_gather(w_mine, 'dp', axis=0, tiled=True)  54.2 us
    dot_general x2, matrix products, contract_rows(): lax.dot_general(left, right, (((0,), (0,)), ((), ())), preferred_element_...  11.3 us
  transfers between devices with their start and end apart: 2, of which 2 were waited for; matrix products, arithmetic and copies ran while one was open for 2% of the time, Pallas kernels for 1%

commit v1 on v0

--- a/solution.py
+++ b/solution.py
@@ -457,9 +457,680 @@
     return (grads[None], grad_first[None], grad_out[None])
 
 
+CORES = 2
+
+
+class Place:
+    def __init__(self):
+        self.pipe, self.dp = lax.axis_index("pipe"), lax.axis_index("dp")
+        self.x, self.core = self.pipe // CORES, self.pipe % CORES
+        self.z, self.y = self.dp // CORES, self.dp % CORES
+
+    def device(self, x=None, core=None, z=None, y=None, pipe=None):
+        x = self.x if x is None else x
+        core = self.core if core is None else core
+        z = self.z if z is None else z
+        y = self.y if y is None else y
+        return {"pipe": x * CORES + core if pipe is None else pipe, "dp": z * CORES + y}
+
+
+def signal(sem, device):
+    pl.semaphore_signal(sem, inc=1, device_id=device, device_id_type=MESH)
+
+
+def remote(src, dst, send, recv, device):
+    return pltpu.make_async_remote_copy(
+        src_ref=src, dst_ref=dst, send_sem=send, recv_sem=recv, device_id=device, device_id_type=MESH
+    )
+
+
+def either(local_if, local, far):
+    pl.when(local_if)(local)
+    pl.when(jnp.logical_not(local_if))(far)
+
+
+def layer_order(step, z, layers):
+    return jnp.where(2 * z < layers, (z + step) % layers, (z + layers - step) % layers)
+
+
+def work_kernel(
+    micro, length, layers,
+    input_ref, top_ref, w_in_ref, w_out_ref, home_mask_ref,
+    grads_ref, up_ref, gpre_ref, normed_ref, gated_ref,
+    first, second, stage_first, stage_second, work_in, top, mask,
+    pre, act, score, unit, rstd, mixed, landed, leaving, ggate, dmix, gnorm,
+    swap_send, swap_recv, top_send, top_recv, pre_send, pre_recv, own_send, hop_send, to_core, to_x, to_y, came,
+    chain_send, chain_recv, back_send, back_recv,
+):
+    me = Place()
+    width = work_in.shape[1]
+    tokens = micro * length
+    section = me.z
+    other_x, other_core, other_y = 1 - me.x, 1 - me.core, 1 - me.y
+    at_home = me.pipe == me.z
+    is_last, is_first = section == layers - 1, section == 0
+    weights = (
+        (w_in_ref, first, stage_first),
+        (w_out_ref, second, stage_second),
+    )
+    sizes = [ref.shape[0] // 4 for ref, _, _ in weights]
+
+    def quarter(which, block, half, core):
+        size = sizes[which]
+        start = pl.multiple_of(((block * 2 + half) * CORES + core) * size, size)
+        return weights[which][1].at[pl.ds(start, size), :]
+
+    def shard(which, half, core):
+        size = sizes[which]
+        start = pl.multiple_of((half * CORES + core) * size, size)
+        return weights[which][0].at[pl.ds(start, size), :]
+
+    def came_at(which, block, half, core):
+        return came.at[which, (block * 2 + half) * CORES + core]
+
+    barrier = pltpu.get_barrier_semaphore()
+    for layer in range(layers):
+        for core in range(CORES):
+
+            @pl.when(jnp.logical_not(jnp.logical_and(layer == me.z, core == me.core)))
+            def _():
+                signal(barrier, me.device(core=core, z=layer))
+
+    for core in range(CORES):
+        signal(barrier, me.device(x=other_x, core=core))
+    signal(barrier, me.device(y=other_y))
+
+    @pl.when(jnp.logical_not(at_home))
+    def _():
+        signal(barrier, {"pipe": me.z, "dp": me.pipe * CORES + me.y})
+
+    pl.semaphore_wait(barrier, layers * CORES + 2 + jnp.where(at_home, 0, 1))
+
+    swap = {"pipe": me.z, "dp": me.pipe * CORES + me.y}
+    swaps = ((input_ref, work_in), (home_mask_ref, mask))
+
+    def swap_far(index):
+        src, dst = swaps[index]
+        return remote(src, dst, swap_send.at[index], swap_recv.at[index], swap)
+
+    def swap_near(index):
+        src, dst = swaps[index]
+        return pltpu.make_async_copy(src, dst, swap_recv.at[index])
+
+    for index in range(2):
+        either(at_home, lambda: swap_near(index).start(), lambda: swap_far(index).start())
+
+    def before(which, core):
+        return remote(
+            shard(which, other_x, core), weights[which][2].at[me.core],
+            pre_send.at[which, core], pre_recv.at[which, me.core], me.device(x=other_x, core=core),
+        )
+
+    def own(which, core):
+        return remote(
+            shard(which, me.x, core), quarter(which, me.dp, me.x, core),
+            own_send.at[which, core], came_at(which, me.dp, me.x, core), me.device(core=core, z=me.pipe),
+        )
+
+    def own_near(which, core):
+        return pltpu.make_async_copy(
+            shard(which, me.x, core), quarter(which, me.dp, me.x, core), came_at(which, me.dp, me.x, core)
+        )
+
+    def hop(which, source):
+        return remote(
+            weights[which][2].at[source], quarter(which, me.dp, me.x, me.core),
+            hop_send.at[which, source], came_at(which, me.dp, me.x, me.core),
+            me.device(z=other_x * CORES + source),
+        )
+
+    def hop_near(which, source):
+        return pltpu.make_async_copy(
+            weights[which][2].at[source], quarter(which, me.dp, me.x, me.core),
+            came_at(which, me.dp, me.x, me.core),
+        )
+
+    def before_came(which, source):
+        return remote(
+            shard(which, other_x, me.core), weights[which][2].at[source],
+            pre_send.at[which, source], pre_recv.at[which, source], me.device(x=other_x),
+        )
+
+    for which in range(2):
+        for core in range(CORES):
+            before(which, core).start()
+        for core in range(CORES):
+            near = jnp.logical_and(at_home, core == me.core)
+            either(near, lambda: own_near(which, core).start(), lambda: own(which, core).start())
+
+    for which in range(2):
+        for source in range(CORES):
+            before_came(which, source).wait_recv()
+            either(
+                other_x * CORES + source == me.z,
+                lambda: hop_near(which, source).start(),
+                lambda: hop(which, source).start(),
+            )
+
+    top_far = remote(top_ref, top, top_send, top_recv, me.device(z=layers - 1))
+    top_near = pltpu.make_async_copy(top_ref, top, top_recv)
+    gives_top = jnp.logical_and(at_home, me.pipe < layers - 1)
+    keeps_top = jnp.logical_and(at_home, me.pipe == layers - 1)
+
+    @pl.when(gives_top)
+    def _():
+        top_far.start()
+
+    @pl.when(keeps_top)
+    def _():
+        top_near.start()
+
+    def send(which, block, half, core, sem, index, device):
+        place = quarter(which, block, half, core)
+        return remote(place, place, sem.at[which, index], came_at(which, block, half, core), device)
+
+    def direct_block(step):
+        return layer_order(step, me.z, layers) * CORES + me.y
+
+    def core_copy(which, kind, step):
+        block = direct_block(step)
+        lane = kind // 2
+        block = block if lane == 0 else block - me.y + other_y
+        half = me.x if kind % 2 == 0 else other_x
+        return send(which, block, half, me.core, to_core, kind * layers + step, me.device(core=other_core))
+
+    def x_copy(which, step):
+        return send(which, direct_block(step), me.x, me.core, to_x, step, me.device(x=other_x))
+
+    def y_copy(which, kind, step):
+        half = me.x if kind == 0 else other_x
+        return send(which, direct_block(step), half, me.core, to_y, kind * layers + step, me.device(y=other_y))
+
+    def arrived(which, block, half, core):
+        place = quarter(which, block, half, core)
+        return remote(
+            place, place, to_core.at[which, 0], came_at(which, block, half, core), me.device(core=other_core)
+        )
+
+    def direct_near(which, step):
+        block = direct_block(step)
+        own_half = me.pipe // CORES == me.z // CORES
+        return own_half, block
+
+    for which in range(2):
+        for step in range(layers + 2):
+            if step < layers:
+                block = direct_block(step)
+                if step == 0:
+                    far = jnp.logical_and(me.x == me.z // CORES, me.core != me.z % CORES)
+                    place = quarter(which, block, me.x, me.core)
+                    either(
+                        jnp.logical_not(far),
+                        lambda: pltpu.make_async_copy(
+                            shard(which, 0, 0), place, came_at(which, block, me.x, me.core)
+                        ).wait(),
+                        lambda: arrived(which, block, me.x, me.core).wait_recv(),
+                    )
+                else:
+                    arrived(which, block, me.x, me.core).wait_recv()
+                x_copy(which, step).start()
+                y_copy(which, 0, step).start()
+                core_copy(which, 0, step).start()
+            if 1 <= step <= layers:
+                block = direct_block(step - 1)
+                arrived(which, block, other_x, me.core).wait_recv()
+                y_copy(which, 1, step - 1).start()
+                core_copy(which, 1, step - 1).start()
+                arrived(which, block - me.y + other_y, me.x, me.core).wait_recv()
+                core_copy(which, 2, step - 1).start()
+            if step >= 2:
+                block = direct_block(step - 2)
+                arrived(which, block - me.y + other_y, other_x, me.core).wait_recv()
+                core_copy(which, 3, step - 2).start()
+
+    for index in range(2):
+        either(at_home, lambda: swap_near(index).wait(), lambda: swap_far(index).wait_recv())
+
+    for which in range(2):
+        def landed_all(index, _):
+            block, half = index // 2, index % 2
+            arrived(which, block, half, other_core).wait_recv()
+            return 0
+
+        lax.fori_loop(0, 2 * layers * CORES, landed_all, 0)
+
+    normed_ref[...] = norm_rows(work_in[...].astype(jnp.float32)).astype(jnp.bfloat16)
+    tile = 2 * LANES
+
+    def front(index, _):
+        cols = at(index * tile, tile)
+        value = dot_nn(normed_ref[...], first[:, cols])
+        pre[:, cols] = value
+        act[:, cols] = jax.nn.silu(value).astype(jnp.bfloat16)
+        return 0
+
+    lax.fori_loop(0, pre.shape[1] // tile, front, 0)
+
+    attend_kernel(micro, length, act, mask, score, unit, rstd, gated_ref, mixed)
+
+    def copy_of(slot):
+        return remote(
+            leaving.at[slot], landed.at[slot], chain_send.at[slot], chain_recv.at[slot],
+            me.device(z=jnp.maximum(me.z - 1, 0)),
+        )
+
+    def back_rows(ref, slot):
+        return ref.at[pl.ds(slot * length, length), :]
+
+    def back_far(slot):
+        return remote(leaving.at[slot], back_rows(grads_ref, slot), back_send.at[slot], back_recv.at[slot], swap)
+
+    def back_near(slot):
+        return pltpu.make_async_copy(leaving.at[slot], back_rows(grads_ref, slot), back_recv.at[slot])
+
+    @pl.when(jnp.logical_and(is_last, jnp.logical_not(at_home)))
+    def _():
+        top_far.wait_recv()
+
+    @pl.when(keeps_top)
+    def _():
+        top_near.wait()
+
+    chain_steps(
+        micro, length, is_first, is_last, copy_of, back_far, back_near, at_home,
+        top, work_in, act, pre, score, unit, rstd, mask, first, second,
+        up_ref, gpre_ref, landed, leaving, ggate, dmix, gnorm,
+    )
+
+    for slot in range(micro):
+
+        @pl.when(jnp.logical_not(is_first))
+        def _():
+            copy_of(slot).wait_send()
+
+        either(at_home, lambda: back_near(slot).wait(), lambda: back_far(slot).wait())
+
+    for index in range(2):
+        pl.when(jnp.logical_not(at_home))(lambda: swap_far(index).wait_send())
+    pl.when(gives_top)(lambda: top_far.wait_send())
+    for which in range(2):
+        for core in range(CORES):
+            before(which, core).wait_send()
+            near = jnp.logical_and(at_home, core == me.core)
+            pl.when(jnp.logical_not(near))(lambda: own(which, core).wait_send())
+        for source in range(CORES):
+            near = other_x * CORES + source == me.z
+            pl.when(jnp.logical_not(near))(lambda: hop(which, source).wait_send())
+
+        def sent(step, _):
+            x_copy(which, step).wait_send()
+            for kind in range(2):
+                y_copy(which, kind, step).wait_send()
+            for kind in range(4):
+                core_copy(which, kind, step).wait_send()
+            return 0
+
+        lax.fori_loop(0, layers, sent, 0)
+
+
+def chain_steps(
+    micro, length, is_first, is_last, copy_of, back_far, back_near, at_home,
+    top_ref, input_ref, act_ref, pre_ref, score_ref, unit_ref, rstd_ref, mask_ref, first_ref, second_ref,
+    up_ref, gpre_ref, landed, leaving, ggate, dmix, gnorm,
+):
+    width = input_ref.shape[1]
+    tile = 2 * LANES
+    lane = lax.broadcasted_iota(jnp.int32, (length, LANES), 1)
+
+    def store_grad(rows, cols, size, value):
+        rounded = value.astype(jnp.bfloat16).astype(jnp.float32)
+        gpre_ref[rows, at(cols, size)] = (
+            rounded * silu_slope(pre_ref[rows, at(cols, size)])
+        ).astype(jnp.bfloat16)
+
+    for slot in range(micro):
+        rows = pl.ds(slot * length, length)
+
+        @pl.when(is_last)
+        def _():
+            up_ref[rows, :] = top_ref[rows, :]
+
+        @pl.when(jnp.logical_not(is_last))
+        def _():
+            copy_of(slot).wait_recv()
+            up_ref[rows, :] = landed[slot]
+
+        def gate_tile(index, _):
+            ggate[:, at(index * tile, tile)] = dot_nt(up_ref[rows, :], second_ref[at(index * tile, tile), :])
+            return 0
+
+        lax.fori_loop(0, V_COLS // tile, gate_tile, 0)
+        gating = act_ref[rows, :V_COLS].astype(jnp.float32)
+        unit = unit_ref[rows, :]
+        grad = ggate[...]
+        store_grad(rows, 0, V_COLS, grad * unit)
+        grad = grad * gating
+        mean_grad = jnp.mean(grad, axis=-1, keepdims=True)
+        mean_unit = jnp.mean(grad * unit, axis=-1, keepdims=True)
+        dmix[...] = (rstd_ref[rows, :1] * (grad - mean_grad - unit * mean_unit)).astype(jnp.bfloat16)
+
+        def one(group, _):
+            queries = act_ref[rows, at(2 * V_COLS + group * LANES, LANES)]
+            keys = act_ref[rows, at(2 * V_COLS + Q_COLS + group * LANES, LANES)]
+            mask = mask_ref[rows, :]
+            grad_q = jnp.zeros((length, LANES), jnp.float32)
+            grad_k = jnp.zeros((length, LANES), jnp.float32)
+            for half in range(GROUP_V // LANES):
+                cols = group * GROUP_V + half * LANES
+                values = act_ref[rows, at(V_COLS + cols, LANES)]
+                grad_mix = dmix[:, at(cols, LANES)]
+                grad_v = jnp.zeros((length, LANES), jnp.float32)
+                for sub in range(V_HEADS):
+                    head = half * V_HEADS + sub
+                    mix_head = only_head(grad_mix, lane, V_DIM, sub)
+                    place = (slot * HEADS + group * QK_HEADS + head) * length
+                    score = score_ref[at(place, length), :]
+                    squash = jax.nn.sigmoid(score)
+                    weight = (score * squash * mask).astype(jnp.bfloat16)
+                    slope = squash * (1.0 + score * (1.0 - squash)) * mask * SCALE
+                    grad_score = (dot_nt(mix_head, values) * slope).astype(jnp.bfloat16)
+                    grad_v += contract_rows(weight, mix_head)
+                    grad_q += dot_nn(grad_score, only_head(keys, lane, QK_DIM, head))
+                    grad_k += contract_rows(grad_score, only_head(queries, lane, QK_DIM, head))
+                store_grad(rows, V_COLS + cols, LANES, grad_v)
+            store_grad(rows, 2 * V_COLS + group * LANES, LANES, grad_q)
+            store_grad(rows, 2 * V_COLS + Q_COLS + group * LANES, LANES, grad_k)
+            return 0
+
+        lax.fori_loop(0, GROUPS, one, 0)
+
+        def norm_tile(index, _):
+            gnorm[:, at(index * tile, tile)] = dot_nt(gpre_ref[rows, :], first_ref[at(index * tile, tile), :])
+            return 0
+
+        lax.fori_loop(0, width // tile, norm_tile, 0)
+        value = input_ref[rows, :].astype(jnp.float32)
+        center = value - jnp.mean(value, axis=-1, keepdims=True)
+        rstd = lax.rsqrt(jnp.mean(center * center, axis=-1, keepdims=True) + EPSILON)
+        unit = center * rstd
+        grad = gnorm[...]
+        mean_grad = jnp.mean(grad, axis=-1, keepdims=True)
+        mean_unit = jnp.mean(grad * unit, axis=-1, keepdims=True)
+        through = rstd * (grad - mean_grad - unit * mean_unit)
+        leaving[slot] = (up_ref[rows, :].astype(jnp.float32) + through).astype(jnp.bfloat16)
+
+        @pl.when(jnp.logical_not(is_first))
+        def _():
+            copy_of(slot).start()
+
+        either(at_home, lambda: back_near(slot).start(), lambda: back_far(slot).start())
+
+
+ANY = pl.BlockSpec(memory_space=pl.ANY)
+LIMIT = 60 * 1024 * 1024
+
+
+def work(inputs, top_grad, w_in, w_out, mask, micro, length):
+    tokens, width = inputs.shape
+    layers, blocks = lax.axis_size("pipe"), lax.axis_size("dp")
+    columns = w_in.shape[1]
+    quarters = [w.shape[0] // 4 for w in (w_in, w_out)]
+    dma = pltpu.SemaphoreType.DMA
+    return pl.pallas_call(
+        functools.partial(work_kernel, micro, length, layers),
+        out_shape=(
+            jax.ShapeDtypeStruct((tokens, width), jnp.bfloat16),
+            jax.ShapeDtypeStruct((tokens, width), jnp.bfloat16),
+            jax.ShapeDtypeStruct((tokens, columns), jnp.bfloat16),
+            jax.ShapeDtypeStruct((tokens, width), jnp.bfloat16),
+            jax.ShapeDtypeStruct((tokens, V_COLS), jnp.bfloat16),
+        ),
+        in_specs=[ANY] * 5,
+        out_specs=(ANY,) + (VMEM,) * 4,
+        scratch_shapes=[
+            pltpu.VMEM((blocks * w_in.shape[0], columns), jnp.bfloat16),
+            pltpu.VMEM((blocks * w_out.shape[0], width), jnp.bfloat16),
+            pltpu.VMEM((CORES, quarters[0], columns), jnp.bfloat16),
+            pltpu.VMEM((CORES, quarters[1], width), jnp.bfloat16),
+            pltpu.VMEM((tokens, width), jnp.bfloat16),
+            pltpu.VMEM((tokens, width), jnp.bfloat16),
+            pltpu.VMEM((tokens, length), jnp.float32),
+            pltpu.VMEM((tokens, columns), jnp.float32),
+            pltpu.VMEM((tokens, columns), jnp.bfloat16),
+            pltpu.VMEM((micro * HEADS * length, length), jnp.float32),
+            pltpu.VMEM((tokens, V_COLS), jnp.float32),
+            pltpu.VMEM((tokens, LANES), jnp.float32),
+            pltpu.VMEM((tokens, V_COLS), jnp.float32),
+            pltpu.VMEM((micro, length, width), jnp.bfloat16),
+            pltpu.VMEM((micro, length, width), jnp.bfloat16),
+            pltpu.VMEM((length, V_COLS), jnp.float32),
+            pltpu.VMEM((length, V_COLS), jnp.bfloat16),
+            pltpu.VMEM((length, width), jnp.float32),
+            dma((2,)), dma((2,)), dma, dma,
+            dma((2, CORES)), dma((2, CORES)), dma((2, CORES)), dma((2, CORES)),
+            dma((2, 4 * layers)), dma((2, layers)), dma((2, 2 * layers)), dma((2, 4 * blocks)),
+            dma((micro,)), dma((micro,)), dma((micro,)), dma((micro,)),
+        ],
+        compiler_params=pltpu.CompilerParams(collective_id=2, has_side_effects=True, vmem_limit_bytes=LIMIT),
+        name="work",
+    )(inputs, top_grad, w_in, w_out, mask)
+
+
+def add_rows(target, other):
+    step = 16
+
+    def one(index, _):
+        rows = pl.ds(pl.multiple_of(index * step, step), step)
+        total = target[rows, :].astype(jnp.float32) + other[rows, :].astype(jnp.float32)
+        target[rows, :] = total.astype(target.dtype)
+        return 0
+
+    lax.fori_loop(0, target.shape[0] // step, one, 0)
+
+
+def weight_kernel(
+    layers,
+    normed_ref, gpre_ref, gated_ref, up_ref,
+    out_first, out_second,
+    first, second, core_first, core_second, y_first, y_second, x_first, x_second,
+    core_send, core_recv, y_send, y_recv, x_send, x_recv, home_send, home_recv,
+):
+    me = Place()
+    other_x, other_core, other_y = 1 - me.x, 1 - me.core, 1 - me.y
+    at_home = me.pipe == me.z
+    sets = (
+        (normed_ref, gpre_ref, out_first, first, core_first, y_first, x_first),
+        (gated_ref, up_ref, out_second, second, core_second, y_second, x_second),
+    )
+    sizes = [s[2].shape[0] // 4 for s in sets]
+
+    barrier = pltpu.get_barrier_semaphore()
+    signal(barrier, me.device(core=other_core))
+    signal(barrier, me.device(x=other_x))
+    signal(barrier, me.device(y=other_y))
+    for pipe in range(layers):
+
+        @pl.when(jnp.logical_not(jnp.logical_and(at_home, pipe == me.pipe)))
+        def _():
+            signal(barrier, {"pipe": pipe, "dp": me.pipe * CORES + me.y})
+
+    pl.semaphore_wait(barrier, 3 + layers - jnp.where(at_home, 1, 0))
+
+    def quarter(which, block, half, core):
+        size = sizes[which]
+        start = pl.multiple_of(((block * 2 + half) * CORES + core) * size, size)
+        return sets[which][3].at[pl.ds(start, size), :]
+
+    def core_copy(which, block, half, mine):
+        core = me.core if mine else other_core
+        index = block * 2 + half
+        return remote(
+            quarter(which, block, half, core), sets[which][4].at[index],
+            core_send.at[which, index], core_recv.at[which, index], me.device(core=other_core),
+        )
+
+    def y_copy(which, row, half, mine):
+        block = row * CORES + (me.y if mine else other_y)
+        index = row * 2 + half
+        return remote(
+            quarter(which, block, half, me.core), sets[which][5].at[index],
+            y_send.at[which, index], y_recv.at[which, index], me.device(y=other_y),
+        )
+
+    def x_copy(which, row, mine):
+        block = row * CORES + me.y
+        return remote(
+            quarter(which, block, me.x if mine else other_x, me.core), sets[which][6].at[row],
+            x_send.at[which, row], x_recv.at[which, row], me.device(x=other_x),
+        )
+
+    def home_rows(which, half, core):
+        size = sizes[which]
+        return sets[which][2].at[pl.ds(pl.multiple_of((half * CORES + core) * size, size), size), :]
+
+    def home_copy(which, row):
+        return remote(
+            quarter(which, row * CORES + me.y, me.x, me.core), home_rows(which, me.x, me.core),
+            home_send.at[which, row], home_recv.at[which, me.x * CORES + me.core],
+            {"pipe": me.z, "dp": row * CORES + me.y},
+        )
+
+    def home_near(which):
+        return pltpu.make_async_copy(
+            quarter(which, me.dp, me.x, me.core), home_rows(which, me.x, me.core),
+            home_recv.at[which, me.x * CORES + me.core],
+        )
+
+    def row_at(step):
+        return layer_order(layers - 1 - step, me.z, layers)
+
+    def product(which, row):
+        left, right, _, whole = sets[which][:4]
+        size = 4 * sizes[which]
+        tile = 2 * LANES
+        for lane_of in (other_y, me.y):
+            block = row * CORES + lane_of
+            place = pl.ds(pl.multiple_of(block * size, size), size)
+
+            def one(index, _):
+                cols = at(index * tile, tile)
+                whole[place, cols] = contract_rows(left[:, place], right[:, cols]).astype(whole.dtype)
+                return 0
+
+            lax.fori_loop(0, right.shape[1] // tile, one, 0)
+            for half in range(2):
+                core_copy(which, block, half, False).start()
+
+    def fold_y(which, row):
+        for half in range(2):
+            block = row * CORES + other_y
+            core_copy(which, block, half, True).wait_recv()
+            add_rows(quarter(which, block, half, me.core), sets[which][4].at[block * 2 + half])
+            y_copy(which, row, half, False).start()
+
+    def fold_x(which, row):
+        for half in (other_x, me.x):
+            block = row * CORES + me.y
+            core_copy(which, block, half, True).wait_recv()
+            place = quarter(which, block, half, me.core)
+            add_rows(place, sets[which][4].at[block * 2 + half])
+            y_copy(which, row, half, True).wait_recv()
+            add_rows(place, sets[which][5].at[row * 2 + half])
+
+            @pl.when(half == other_x)
+            def _():
+                x_copy(which, row, False).start()
+
+    def fold_home(which, row):
+        x_copy(which, row, True).wait_recv()
+        add_rows(quarter(which, row * CORES + me.y, me.x, me.core), sets[which][6].at[row])
+        near = jnp.logical_and(at_home, row == me.z)
+        either(near, lambda: home_near(which).start(), lambda: home_copy(which, row).start())
+
+    def run(step, _):
+        for which in range(2):
+
+            @pl.when(step < layers)
+            def _():
+                product(which, row_at(step))
+
+            @pl.when(jnp.logical_and(step >= 1, step < layers + 1))
+            def _():
+                fold_y(which, row_at(step - 1))
+
+            @pl.when(jnp.logical_and(step >= 2, step < layers + 2))
+            def _():
+                fold_x(which, row_at(step - 2))
+
+            @pl.when(step >= 3)
+            def _():
+                fold_home(which, row_at(step - 3))
+
+        return 0
+
+    lax.fori_loop(0, layers + 3, run, 0)
+
+    for which in range(2):
+        for pipe in range(layers):
+            place = home_rows(which, pipe // CORES, pipe % CORES)
+            near = jnp.logical_and(at_home, pipe == me.pipe)
+            either(
+                near,
+                lambda: home_near(which).wait(),
+                lambda: remote(
+                    place, place, home_send.at[which, 0], home_recv.at[which, pipe], me.device(core=other_core)
+                ).wait_recv(),
+            )
+
+        def sent(row, _):
+            for half in range(2):
+                for lane_of in range(2):
+                    core_copy(which, row * CORES + lane_of, half, False).wait_send()
+                y_copy(which, row, half, False).wait_send()
+            x_copy(which, row, False).wait_send()
+            near = jnp.logical_and(at_home, row == me.z)
+            pl.when(jnp.logical_not(near))(lambda: home_copy(which, row).wait_send())
+            return 0
+
+        lax.fori_loop(0, layers, sent, 0)
+
+
+def weight_sums(normed, grad_preact, gated, upstream):
+    layers, blocks = lax.axis_size("pipe"), lax.axis_size("dp")
+    dma = pltpu.SemaphoreType.DMA
+    pairs = ((normed, grad_preact), (gated, upstream))
+    shapes = [(left.shape[1], right.shape[1]) for left, right in pairs]
+    scratch = [pltpu.VMEM(shape, jnp.bfloat16) for shape in shapes]
+    for count in (2 * blocks, 2 * layers, layers):
+        for rows, cols in shapes:
+            scratch.append(pltpu.VMEM((count, rows // (4 * blocks), cols), jnp.bfloat16))
+    for count in (2 * blocks, 2 * layers, layers, layers):
+        scratch += [dma((2, count))] * 2
+    return pl.pallas_call(
+        functools.partial(weight_kernel, layers),
+        out_shape=tuple(jax.ShapeDtypeStruct((rows // blocks, cols), jnp.bfloat16) for rows, cols in shapes),
+        in_specs=[VMEM] * 4,
+        out_specs=(ANY,) * 2,
+        scratch_shapes=scratch,
+        compiler_params=pltpu.CompilerParams(collective_id=3, has_side_effects=True, vmem_limit_bytes=LIMIT),
+        name="weight_sums",
+    )(normed, grad_preact, gated, upstream)
+
+
+def layered_body(section_input, top_grad, w_in, w_out, segments):
+    micro, length = segments.shape
+    mask = mask_of(segments)
+    grads, upstream, grad_preact, normed, gated = work(
+        section_input[0], top_grad, w_in[0], w_out[0], mask, micro, length
+    )
+    grad_first, grad_out = weight_sums(normed, grad_preact, gated, upstream)
+    return (grads[None], grad_first.astype(jnp.float32)[None], grad_out.astype(jnp.float32)[None])
+
+
 def solution(mesh):
+    layered = mesh.shape["pipe"] == CORES * 2 and mesh.shape["dp"] == CORES * mesh.shape["pipe"]
     return jax.shard_map(
-        body,
+        layered_body if layered else body,
         mesh=mesh,
         in_specs=(
             P("pipe", "dp", None),

time: 540 us -> 427 us (0.79)
  waiting for transfers between devices: 234 us -> 0 us
  Pallas kernels: 261 us -> 413 us
  matrix products: 21.5 us -> 0 us
  between operations: 14.1 us -> 0.67 us
    all_gather x2 -> x0, waiting for transfers between devices: 233 us -> none  [the longest x1 179 us: body(): w_first = lax.all_gather(w_in[0], 'dp', axis=0, tiled=True)]
    pallas_call x3 -> x2, Pallas kernels: 261 us -> 413 us  [the longest x1 284 us: work(): pl.pallas_call(functools.partial(work_kernel, micro, length, layers), out...]
    dot_general x3 -> x0, matrix products: 21.5 us -> none  [the longest x2 11.3 us: contract_rows(): lax.dot_general(left, right, (((0,), (0,)), ((), ())), preferred_element_...]
  transfers between devices with their start and end apart: 2 -> 0, of which waited for: 2 -> 0; matrix products, arithmetic and copies ran while one was open for 2% -> 0% of each run, Pallas kernels for 1% -> 0%
where the time goes in v1:
time: 427 us; the launch traced here: 422 us
  Pallas kernels  413 us (97%)
  other arithmetic  6.76 us (2%)
    pallas_call x1, Pallas kernels, work(): pl.pallas_call(functools.partial(work_kernel, micro, length, layers), out...  284 us
    pallas_call x1, Pallas kernels, weight_sums(): pl.pallas_call(functools.partial(weight_kernel, layers), out_shape=tuple(...  129 us

profile of v1, /device:TPU:4, one launch (start us, length us, event | category | flops | bytes accessed | tf_op | source)
XLA Modules:
  0.0 421.6 jit_solution(16385331585533981807)
XLA Ops:
  0.6 0.9 convert_reduce_fusion
  1.6 1.6 convert_divide_fusion.home_mask_ref
  3.1 283.8 %work.1 = (bf16[256,2048]{1,0:T(8,128)(2,1)}, bf16[256,2048]{1,0:T(8,128)(2,1)}, bf16[256,3072]{1,0:T(8,128)(2,1)}, bf16[256,2048]{1,0:T(8,128)(2,1)}, bf16[256,1024]{1,0:T(8,128)(2,1)}) custom-call(bf16[256,2048]{1,0:T(8,128)(2,1)} %bitcast.22, bf16[256,2048]{1,0:T(8,128)(2,1)} %top_ref.1, bf16[256,3072]{1,0:T(8,128)(2,1)} %bitcast.20, ...), custom_call_target="tpu_custom_call" | custom-call | tf_op jit(solution)/shard_map/work/pallas_call | solution.py:879
  286.9 129.4 %weight_sums.1 = (bf16[256,3072]{1,0:T(8,128)(2,1)}, bf16[128,2048]{1,0:T(8,128)(2,1)}) custom-call(bf16[256,2048]{1,0:T(8,128)(2,1)} %get-tuple-element.11.normed_ref, bf16[256,3072]{1,0:T(8,128)(2,1)} %get-tuple-element.12.gpre_ref, bf16[256,1024]{1,0:T(8,128)(2,1)} %get-tuple-element.13.gated_ref, bf16[256,2048]{1,0:T(8,128)(2,1)} %get-tuple-element.14.up_ref), custom_call_target="tpu_custom_call" | custom-call | tf_op jit(solution)/shard_map/weight_sums/pallas_call | solution.py:1109
  416.4 0.0 copy-start
  416.4 2.2 bitcast_convert_fusion.1
  418.6 0.0 copy-done
  418.6 0.0 copy-start.1
  418.6 2.0 bitcast_convert_fusion
  420.6 0.0 copy-done.1
  420.6 1.0 copy.9
  (1 shorter events, 0.0 us)
Async XLA Ops:
  416.4 2.2 copy-start
  418.6 2.0 copy-start.1

commit v2 on v1

--- a/solution.py
+++ b/solution.py
@@ -498,9 +498,9 @@
     input_ref, top_ref, w_in_ref, w_out_ref, home_mask_ref,
     grads_ref, up_ref, gpre_ref, normed_ref, gated_ref,
     first, second, stage_first, stage_second, work_in, top, mask,
-    pre, act, score, unit, rstd, mixed, landed, leaving, ggate, dmix, gnorm,
+    unit_in, rstd_in, slope, act, weight, weight_slope, unit, rstd, mixed, landed, ggate, gnorm,
     swap_send, swap_recv, top_send, top_recv, pre_send, pre_recv, own_send, hop_send, to_core, to_x, to_y, came,
-    chain_send, chain_recv, back_send, back_recv,
+    chain_send, chain_recv,
 ):
     me = Place()
     width = work_in.shape[1]
@@ -557,8 +557,9 @@
         src, dst = swaps[index]
         return pltpu.make_async_copy(src, dst, swap_recv.at[index])
 
-    for index in range(2):
-        either(at_home, lambda: swap_near(index).start(), lambda: swap_far(index).start())
+    def swap_start():
+        for index in range(2):
+            either(at_home, lambda: swap_near(index).start(), lambda: swap_far(index).start())
 
     def before(which, core):
         return remote(
@@ -617,13 +618,9 @@
     gives_top = jnp.logical_and(at_home, me.pipe < layers - 1)
     keeps_top = jnp.logical_and(at_home, me.pipe == layers - 1)
 
-    @pl.when(gives_top)
-    def _():
-        top_far.start()
-
-    @pl.when(keeps_top)
-    def _():
-        top_near.start()
+    def top_start():
+        pl.when(gives_top)(lambda: top_far.start())
+        pl.when(keeps_top)(lambda: top_near.start())
 
     def send(which, block, half, core, sem, index, device):
         place = quarter(which, block, half, core)
@@ -652,13 +649,21 @@
             place, place, to_core.at[which, 0], came_at(which, block, half, core), me.device(core=other_core)
         )
 
-    def direct_near(which, step):
-        block = direct_block(step)
-        own_half = me.pipe // CORES == me.z // CORES
-        return own_half, block
-
-    for which in range(2):
-        for step in range(layers + 2):
+    def settled(which):
+        for core in range(CORES):
+            near = jnp.logical_and(at_home, core == me.core)
+            pl.when(jnp.logical_not(near))(lambda: own(which, core).wait_send())
+        for source in range(CORES):
+            near = other_x * CORES + source == me.z
+            pl.when(jnp.logical_not(near))(lambda: hop(which, source).wait_send())
+
+    for step in range(layers + 2):
+        if step == 2:
+            for which in range(2):
+                settled(which)
+            swap_start()
+            top_start()
+        for which in range(2):
             if step < layers:
                 block = direct_block(step)
                 if step == 0:
@@ -676,6 +681,7 @@
                 x_copy(which, step).start()
                 y_copy(which, 0, step).start()
                 core_copy(which, 0, step).start()
+        for which in range(2):
             if 1 <= step <= layers:
                 block = direct_block(step - 1)
                 arrived(which, block, other_x, me.core).wait_recv()
@@ -683,6 +689,7 @@
                 core_copy(which, 1, step - 1).start()
                 arrived(which, block - me.y + other_y, me.x, me.core).wait_recv()
                 core_copy(which, 2, step - 1).start()
+        for which in range(2):
             if step >= 2:
                 block = direct_block(step - 2)
                 arrived(which, block - me.y + other_y, other_x, me.core).wait_recv()
@@ -699,34 +706,25 @@
 
         lax.fori_loop(0, 2 * layers * CORES, landed_all, 0)
 
-    normed_ref[...] = norm_rows(work_in[...].astype(jnp.float32)).astype(jnp.bfloat16)
+    norm_input(work_in, normed_ref, unit_in, rstd_in)
     tile = 2 * LANES
 
     def front(index, _):
         cols = at(index * tile, tile)
         value = dot_nn(normed_ref[...], first[:, cols])
-        pre[:, cols] = value
-        act[:, cols] = jax.nn.silu(value).astype(jnp.bfloat16)
+        squash = jax.nn.sigmoid(value)
+        act[:, cols] = (value * squash).astype(jnp.bfloat16)
+        slope[:, cols] = squash * (1.0 + value * (1.0 - squash))
         return 0
 
-    lax.fori_loop(0, pre.shape[1] // tile, front, 0)
-
-    attend_kernel(micro, length, act, mask, score, unit, rstd, gated_ref, mixed)
+    lax.fori_loop(0, slope.shape[1] // tile, front, 0)
+    attend_front(micro, length, act, mask, weight, weight_slope, unit, rstd, gated_ref, mixed)
 
     def copy_of(slot):
         return remote(
-            leaving.at[slot], landed.at[slot], chain_send.at[slot], chain_recv.at[slot],
+            grads_ref.at[pl.ds(slot * length, length), :], landed.at[slot], chain_send.at[slot], chain_recv.at[slot],
             me.device(z=jnp.maximum(me.z - 1, 0)),
         )
-
-    def back_rows(ref, slot):
-        return ref.at[pl.ds(slot * length, length), :]
-
-    def back_far(slot):
-        return remote(leaving.at[slot], back_rows(grads_ref, slot), back_send.at[slot], back_recv.at[slot], swap)
-
-    def back_near(slot):
-        return pltpu.make_async_copy(leaving.at[slot], back_rows(grads_ref, slot), back_recv.at[slot])
 
     @pl.when(jnp.logical_and(is_last, jnp.logical_not(at_home)))
     def _():
@@ -737,9 +735,9 @@
         top_near.wait()
 
     chain_steps(
-        micro, length, is_first, is_last, copy_of, back_far, back_near, at_home,
-        top, work_in, act, pre, score, unit, rstd, mask, first, second,
-        up_ref, gpre_ref, landed, leaving, ggate, dmix, gnorm,
+        micro, length, is_first, is_last, copy_of,
+        top, unit_in, rstd_in, act, slope, weight, weight_slope, unit, rstd, first, second,
+        grads_ref, up_ref, gpre_ref, landed, ggate, gnorm,
     )
 
     for slot in range(micro):
@@ -747,8 +745,6 @@
         @pl.when(jnp.logical_not(is_first))
         def _():
             copy_of(slot).wait_send()
-
-        either(at_home, lambda: back_near(slot).wait(), lambda: back_far(slot).wait())
 
     for index in range(2):
         pl.when(jnp.logical_not(at_home))(lambda: swap_far(index).wait_send())
@@ -756,11 +752,6 @@
     for which in range(2):
         for core in range(CORES):
             before(which, core).wait_send()
-            near = jnp.logical_and(at_home, core == me.core)
-            pl.when(jnp.logical_not(near))(lambda: own(which, core).wait_send())
-        for source in range(CORES):
-            near = other_x * CORES + source == me.z
-            pl.when(jnp.logical_not(near))(lambda: hop(which, source).wait_send())
 
         def sent(step, _):
             x_copy(which, step).wait_send()
@@ -773,20 +764,86 @@
         lax.fori_loop(0, layers, sent, 0)
 
 
+def folded(value):
+    total = value[:, :LANES]
+    for start in range(LANES, value.shape[1], LANES):
+        total = total + value[:, start : start + LANES]
+    return total
+
+
+def norm_input(work_in, normed_ref, unit_in, rstd_in):
+    step = 64
+    width = work_in.shape[1]
+
+    def one(index, _):
+        rows = pl.ds(pl.multiple_of(index * step, step), step)
+        value = work_in[rows, :].astype(jnp.float32)
+        center = value - jnp.mean(value, axis=-1, keepdims=True)
+        rstd = lax.rsqrt(jnp.mean(center * center, axis=-1, keepdims=True) + EPSILON)
+        unit = center * rstd
+        unit_in[rows, :] = unit
+        normed_ref[rows, :] = unit.astype(jnp.bfloat16)
+        rstd_in[rows, :] = jnp.broadcast_to(rstd, (step, LANES))
+        return 0
+
+    lax.fori_loop(0, work_in.shape[0] // step, one, 0)
+
+
+def attend_front(micro, length, act_ref, mask_ref, weight_ref, slope_ref, unit_ref, rstd_ref, gated_ref, mixed):
+    lane = lax.broadcasted_iota(jnp.int32, (length, LANES), 1)
+
+    def one(index, _):
+        slot, group = index // GROUPS, index % GROUPS
+        rows = at(slot * length, length)
+        queries = act_ref[rows, at(2 * V_COLS + group * LANES, LANES)]
+        keys = act_ref[rows, at(2 * V_COLS + Q_COLS + group * LANES, LANES)]
+        mask = mask_ref[rows, :]
+        for half in range(GROUP_V // LANES):
+            cols = group * GROUP_V + half * LANES
+            values = act_ref[rows, at(V_COLS + cols, LANES)]
+            total = jnp.zeros((length, LANES), jnp.float32)
+            for sub in range(V_HEADS):
+                head = half * V_HEADS + sub
+                score = dot_nt(only_head(queries, lane, QK_DIM, head), keys) * SCALE
+                squash = jax.nn.sigmoid(score)
+                place = at((index * QK_HEADS + head) * length, length)
+                slope_ref[place, :] = squash * (1.0 + score * (1.0 - squash)) * (mask * SCALE)
+                weight = (score * squash * mask).astype(jnp.bfloat16)
+                weight_ref[place, :] = weight
+                total += dot_nn(weight, only_head(values, lane, V_DIM, sub))
+            mixed[rows, at(cols, LANES)] = total
+        return 0
+
+    lax.fori_loop(0, micro * GROUPS, one, 0)
+    step = 64
+
+    def finish(index, _):
+        rows = pl.ds(pl.multiple_of(index * step, step), step)
+        value = mixed[rows, :]
+        center = value - jnp.mean(value, axis=-1, keepdims=True)
+        rstd = lax.rsqrt(jnp.mean(center * center, axis=-1, keepdims=True) + EPSILON)
+        unit = center * rstd
+        unit_ref[rows, :] = unit
+        rstd_ref[rows, :] = jnp.broadcast_to(rstd, (step, LANES))
+        gated_ref[rows, :] = (unit * act_ref[rows, :V_COLS].astype(jnp.float32)).astype(jnp.bfloat16)
+        return 0
+
+    lax.fori_loop(0, micro * length // step, finish, 0)
+
+
 def chain_steps(
-    micro, length, is_first, is_last, copy_of, back_far, back_near, at_home,
-    top_ref, input_ref, act_ref, pre_ref, score_ref, unit_ref, rstd_ref, mask_ref, first_ref, second_ref,
-    up_ref, gpre_ref, landed, leaving, ggate, dmix, gnorm,
+    micro, length, is_first, is_last, copy_of,
+    top_ref, unit_in, rstd_in, act_ref, slope_ref, weight_ref, weight_slope, unit_ref, rstd_ref, first_ref, second_ref,
+    grads_ref, up_ref, gpre_ref, landed, ggate, gnorm,
 ):
-    width = input_ref.shape[1]
+    width = unit_in.shape[1]
     tile = 2 * LANES
     lane = lax.broadcasted_iota(jnp.int32, (length, LANES), 1)
+    nothing = jnp.zeros((length, LANES), jnp.float32)
 
     def store_grad(rows, cols, size, value):
         rounded = value.astype(jnp.bfloat16).astype(jnp.float32)
-        gpre_ref[rows, at(cols, size)] = (
-            rounded * silu_slope(pre_ref[rows, at(cols, size)])
-        ).astype(jnp.bfloat16)
+        gpre_ref[rows, at(cols, size)] = (rounded * slope_ref[rows, at(cols, size)]).astype(jnp.bfloat16)
 
     for slot in range(micro):
         rows = pl.ds(slot * length, length)
@@ -800,41 +857,36 @@
             copy_of(slot).wait_recv()
             up_ref[rows, :] = landed[slot]
 
-        def gate_tile(index, _):
-            ggate[:, at(index * tile, tile)] = dot_nt(up_ref[rows, :], second_ref[at(index * tile, tile), :])
-            return 0
-
-        lax.fori_loop(0, V_COLS // tile, gate_tile, 0)
-        gating = act_ref[rows, :V_COLS].astype(jnp.float32)
-        unit = unit_ref[rows, :]
-        grad = ggate[...]
-        store_grad(rows, 0, V_COLS, grad * unit)
-        grad = grad * gating
-        mean_grad = jnp.mean(grad, axis=-1, keepdims=True)
-        mean_unit = jnp.mean(grad * unit, axis=-1, keepdims=True)
-        dmix[...] = (rstd_ref[rows, :1] * (grad - mean_grad - unit * mean_unit)).astype(jnp.bfloat16)
+        def gate_tile(index, sums):
+            cols = at(index * tile, tile)
+            grad = dot_nt(up_ref[rows, :], second_ref[cols, :])
+            unit = unit_ref[rows, cols]
+            store_grad(rows, index * tile, tile, grad * unit)
+            grad = grad * act_ref[rows, cols].astype(jnp.float32)
+            ggate[:, cols] = grad
+            return sums[0] + folded(grad), sums[1] + folded(grad * unit)
+
+        sums = lax.fori_loop(0, V_COLS // tile, gate_tile, (nothing, nothing))
+        mean_grad, mean_unit = [jnp.sum(part, axis=-1, keepdims=True) * (1.0 / V_COLS) for part in sums]
+        rstd = rstd_ref[rows, :1]
 
         def one(group, _):
             queries = act_ref[rows, at(2 * V_COLS + group * LANES, LANES)]
             keys = act_ref[rows, at(2 * V_COLS + Q_COLS + group * LANES, LANES)]
-            mask = mask_ref[rows, :]
             grad_q = jnp.zeros((length, LANES), jnp.float32)
             grad_k = jnp.zeros((length, LANES), jnp.float32)
             for half in range(GROUP_V // LANES):
                 cols = group * GROUP_V + half * LANES
                 values = act_ref[rows, at(V_COLS + cols, LANES)]
-                grad_mix = dmix[:, at(cols, LANES)]
+                spread = ggate[:, at(cols, LANES)] - mean_grad - unit_ref[rows, at(cols, LANES)] * mean_unit
+                grad_mix = (rstd * spread).astype(jnp.bfloat16)
                 grad_v = jnp.zeros((length, LANES), jnp.float32)
                 for sub in range(V_HEADS):
                     head = half * V_HEADS + sub
                     mix_head = only_head(grad_mix, lane, V_DIM, sub)
-                    place = (slot * HEADS + group * QK_HEADS + head) * length
-                    score = score_ref[at(place, length), :]
-                    squash = jax.nn.sigmoid(score)
-                    weight = (score * squash * mask).astype(jnp.bfloat16)
-                    slope = squash * (1.0 + score * (1.0 - squash)) * mask * SCALE
-                    grad_score = (dot_nt(mix_head, values) * slope).astype(jnp.bfloat16)
-                    grad_v += contract_rows(weight, mix_head)
+                    place = at((slot * HEADS + group * QK_HEADS + head) * length, length)
+                    grad_score = (dot_nt(mix_head, values) * weight_slope[place, :]).astype(jnp.bfloat16)
+                    grad_v += contract_rows(weight_ref[place, :], mix_head)
                     grad_q += dot_nn(grad_score, only_head(keys, lane, QK_DIM, head))
                     grad_k += contract_rows(grad_score, only_head(queries, lane, QK_DIM, head))
                 store_grad(rows, V_COLS + cols, LANES, grad_v)
@@ -844,26 +896,27 @@
 
         lax.fori_loop(0, GROUPS, one, 0)
 
-        def norm_tile(index, _):
-            gnorm[:, at(index * tile, tile)] = dot_nt(gpre_ref[rows, :], first_ref[at(index * tile, tile), :])
+        def norm_tile(index, sums):
+            cols = at(index * tile, tile)
+            grad = dot_nt(gpre_ref[rows, :], first_ref[cols, :])
+            gnorm[:, cols] = grad
+            return sums[0] + folded(grad), sums[1] + folded(grad * unit_in[rows, cols])
+
+        sums = lax.fori_loop(0, width // tile, norm_tile, (nothing, nothing))
+        mean_grad, mean_unit = [jnp.sum(part, axis=-1, keepdims=True) * (1.0 / width) for part in sums]
+        rstd = rstd_in[rows, :1]
+
+        def pass_tile(index, _):
+            cols = at(index * tile, tile)
+            through = rstd * (gnorm[:, cols] - mean_grad - unit_in[rows, cols] * mean_unit)
+            grads_ref[rows, cols] = (up_ref[rows, cols].astype(jnp.float32) + through).astype(jnp.bfloat16)
             return 0
 
-        lax.fori_loop(0, width // tile, norm_tile, 0)
-        value = input_ref[rows, :].astype(jnp.float32)
-        center = value - jnp.mean(value, axis=-1, keepdims=True)
-        rstd = lax.rsqrt(jnp.mean(center * center, axis=-1, keepdims=True) + EPSILON)
-        unit = center * rstd
-        grad = gnorm[...]
-        mean_grad = jnp.mean(grad, axis=-1, keepdims=True)
-        mean_unit = jnp.mean(grad * unit, axis=-1, keepdims=True)
-        through = rstd * (grad - mean_grad - unit * mean_unit)
-        leaving[slot] = (up_ref[rows, :].astype(jnp.float32) + through).astype(jnp.bfloat16)
+        lax.fori_loop(0, width // tile, pass_tile, 0)
 
         @pl.when(jnp.logical_not(is_first))
         def _():
             copy_of(slot).start()
-
-        either(at_home, lambda: back_near(slot).start(), lambda: back_far(slot).start())
 
 
 ANY = pl.BlockSpec(memory_space=pl.ANY)
@@ -886,7 +939,7 @@
             jax.ShapeDtypeStruct((tokens, V_COLS), jnp.bfloat16),
         ),
         in_specs=[ANY] * 5,
-        out_specs=(ANY,) + (VMEM,) * 4,
+        out_specs=(VMEM,) * 5,
         scratch_shapes=[
             pltpu.VMEM((blocks * w_in.shape[0], columns), jnp.bfloat16),
             pltpu.VMEM((blocks * w_out.shape[0], width), jnp.bfloat16),
@@ -895,21 +948,22 @@
             pltpu.VMEM((tokens, width), jnp.bfloat16),
             pltpu.VMEM((tokens, width), jnp.bfloat16),
             pltpu.VMEM((tokens, length), jnp.float32),
+            pltpu.VMEM((tokens, width), jnp.float32),
+            pltpu.VMEM((tokens, LANES), jnp.float32),
             pltpu.VMEM((tokens, columns), jnp.float32),
             pltpu.VMEM((tokens, columns), jnp.bfloat16),
+            pltpu.VMEM((micro * HEADS * length, length), jnp.bfloat16),
             pltpu.VMEM((micro * HEADS * length, length), jnp.float32),
             pltpu.VMEM((tokens, V_COLS), jnp.float32),
             pltpu.VMEM((tokens, LANES), jnp.float32),
             pltpu.VMEM((tokens, V_COLS), jnp.float32),
             pltpu.VMEM((micro, length, width), jnp.bfloat16),
-            pltpu.VMEM((micro, length, width), jnp.bfloat16),
             pltpu.VMEM((length, V_COLS), jnp.float32),
-            pltpu.VMEM((length, V_COLS), jnp.bfloat16),
             pltpu.VMEM((length, width), jnp.float32),
             dma((2,)), dma((2,)), dma, dma,
             dma((2, CORES)), dma((2, CORES)), dma((2, CORES)), dma((2, CORES)),
             dma((2, 4 * layers)), dma((2, layers)), dma((2, 2 * layers)), dma((2, 4 * blocks)),
-            dma((micro,)), dma((micro,)), dma((micro,)), dma((micro,)),
+            dma((micro,)), dma((micro,)),
         ],
         compiler_params=pltpu.CompilerParams(collective_id=2, has_side_effects=True, vmem_limit_bytes=LIMIT),
         name="work",
@@ -930,10 +984,11 @@
 
 def weight_kernel(
     layers,
-    normed_ref, gpre_ref, gated_ref, up_ref,
-    out_first, out_second,
+    normed_ref, gpre_ref, gated_ref, up_ref, done_ref,
+    out_first, out_second, grads_ref,
     first, second, core_first, core_second, y_first, y_second, x_first, x_second,
     core_send, core_recv, y_send, y_recv, x_send, x_recv, home_send, home_recv,
+    back_send, back_recv,
 ):
     me = Place()
     other_x, other_core, other_y = 1 - me.x, 1 - me.core, 1 - me.y
@@ -956,6 +1011,10 @@
 
     pl.semaphore_wait(barrier, 3 + layers - jnp.where(at_home, 1, 0))
 
+    back_far = remote(done_ref, grads_ref, back_send, back_recv, {"pipe": me.z, "dp": me.pipe * CORES + me.y})
+    back_near = pltpu.make_async_copy(done_ref, grads_ref, back_recv)
+    either(at_home, lambda: back_near.start(), lambda: back_far.start())
+
     def quarter(which, block, half, core):
         size = sizes[which]
         start = pl.multiple_of(((block * 2 + half) * CORES + core) * size, size)
@@ -1069,6 +1128,7 @@
         return 0
 
     lax.fori_loop(0, layers + 3, run, 0)
+    either(at_home, lambda: back_near.wait(), lambda: back_far.wait())
 
     for which in range(2):
         for pipe in range(layers):
@@ -1095,7 +1155,7 @@
         lax.fori_loop(0, layers, sent, 0)
 
 
-def weight_sums(normed, grad_preact, gated, upstream):
+def weight_sums(normed, grad_preact, gated, upstream, grads):
     layers, blocks = lax.axis_size("pipe"), lax.axis_size("dp")
     dma = pltpu.SemaphoreType.DMA
     pairs = ((normed, grad_preact), (gated, upstream))
@@ -1106,15 +1166,17 @@
             scratch.append(pltpu.VMEM((count, rows // (4 * blocks), cols), jnp.bfloat16))
     for count in (2 * blocks, 2 * layers, layers, layers):
         scratch += [dma((2, count))] * 2
+    scratch += [dma, dma]
     return pl.pallas_call(
         functools.partial(weight_kernel, layers),
-        out_shape=tuple(jax.ShapeDtypeStruct((rows // blocks, cols), jnp.bfloat16) for rows, cols in shapes),
-        in_specs=[VMEM] * 4,
-        out_specs=(ANY,) * 2,
+        out_shape=tuple(jax.ShapeDtypeStruct((rows // blocks, cols), jnp.bfloat16) for rows, cols in shapes)
+        + (jax.ShapeDtypeStruct(grads.shape, grads.dtype),),
+        in_specs=[VMEM] * 4 + [ANY],
+        out_specs=(ANY,) * 3,
         scratch_shapes=scratch,
         compiler_params=pltpu.CompilerParams(collective_id=3, has_side_effects=True, vmem_limit_bytes=LIMIT),
         name="weight_sums",
-    )(normed, grad_preact, gated, upstream)
+    )(normed, grad_preact, gated, upstream, grads)
 
 
 def layered_body(section_input, top_grad, w_in, w_out, segments):
@@ -1123,7 +1185,7 @@
     grads, upstream, grad_preact, normed, gated = work(
         section_input[0], top_grad, w_in[0], w_out[0], mask, micro, length
     )
-    grad_first, grad_out = weight_sums(normed, grad_preact, gated, upstream)
+    grad_first, grad_out, grads = weight_sums(normed, grad_preact, gated, upstream, grads)
     return (grads[None], grad_first.astype(jnp.float32)[None], grad_out.astype(jnp.float32)[None])
 
 

time: 427 us -> 380 us (0.89)
  the two profiles are of different devices: /device:TPU:4 before, /device:TPU:22 now
where the time goes in v2:
time: 380 us
  Pallas kernels  372 us (98%)
  other arithmetic  6.76 us (2%)
    pallas_call x1, Pallas kernels, work(): pl.pallas_call(functools.partial(work_kernel, micro, length, layers), out...  196 us
    pallas_call x1, Pallas kernels, weight_sums(): pl.pallas_call(functools.partial(weight_kernel, layers), out_shape=tuple(...  176 us

profile of v2, /device:TPU:22, one launch (start us, length us, event | category | flops | bytes accessed | tf_op | source)
XLA Modules:
  0.0 380.0 jit_solution(1700667040092576622)
XLA Ops:
  0.6 0.9 convert_reduce_fusion
  1.6 1.6 convert_divide_fusion.home_mask_ref
  3.1 195.6 %work.1 = (bf16[256,2048]{1,0:T(8,128)(2,1)}, bf16[256,2048]{1,0:T(8,128)(2,1)}, bf16[256,3072]{1,0:T(8,128)(2,1)}, bf16[256,2048]{1,0:T(8,128)(2,1)}, bf16[256,1024]{1,0:T(8,128)(2,1)}) custom-call(bf16[256,2048]{1,0:T(8,128)(2,1)} %bitcast.22, bf16[256,2048]{1,0:T(8,128)(2,1)} %top_ref.1, bf16[256,3072]{1,0:T(8,128)(2,1)} %bitcast.20, ...), custom_call_target="tpu_custom_call" | custom-call | tf_op jit(solution)/shard_map/work/pallas_call | solution.py:932
  198.7 176.0 %weight_sums.1 = (bf16[256,3072]{1,0:T(8,128)(2,1)}, bf16[128,2048]{1,0:T(8,128)(2,1)}, bf16[256,2048]{1,0:T(8,128)(2,1)}) custom-call(bf16[256,2048]{1,0:T(8,128)(2,1)} %get-tuple-element.11.normed_ref, bf16[256,3072]{1,0:T(8,128)(2,1)} %get-tuple-element.12.gpre_ref, bf16[256,1024]{1,0:T(8,128)(2,1)} %get-tuple-element.13.gated_ref, ...), custom_call_target="tpu_custom_call" | custom-call | tf_op jit(solution)/shard_map/weight_sums/pallas_call | solution.py:1170
  374.7 0.0 copy-start
  374.7 2.2 bitcast_convert_fusion.1
  376.9 0.0 copy-done
  377.0 0.0 copy-start.1
  377.0 2.0 bitcast_convert_fusion
  379.0 0.0 copy-done.1
  379.0 1.0 copy.9
  (1 shorter events, 0.0 us)
Async XLA Ops:
  374.7 2.2 copy-start
  377.0 2.0 copy-start.1

commit v3 on v2

--- a/solution.py
+++ b/solution.py
@@ -489,6 +489,10 @@
     pl.when(jnp.logical_not(local_if))(far)
 
 
+def turned(index):
+    return index % CORES * CORES + index // CORES
+
+
 def layer_order(step, z, layers):
     return jnp.where(2 * z < layers, (z + step) % layers, (z + layers - step) % layers)
 
@@ -496,11 +500,13 @@
 def work_kernel(
     micro, length, layers,
     input_ref, top_ref, w_in_ref, w_out_ref, home_mask_ref,
+    out_first, out_second, out_grads,
     grads_ref, up_ref, gpre_ref, normed_ref, gated_ref,
     first, second, stage_first, stage_second, work_in, top, mask,
     unit_in, rstd_in, slope, act, weight, weight_slope, unit, rstd, mixed, landed, ggate, gnorm,
     swap_send, swap_recv, top_send, top_recv, pre_send, pre_recv, own_send, hop_send, to_core, to_x, to_y, came,
-    chain_send, chain_recv,
+    chain_send, chain_recv, back_send, back_recv,
+    *sums,
 ):
     me = Place()
     width = work_in.shape[1]
@@ -529,29 +535,27 @@
         return came.at[which, (block * 2 + half) * CORES + core]
 
     barrier = pltpu.get_barrier_semaphore()
-    for layer in range(layers):
-        for core in range(CORES):
-
-            @pl.when(jnp.logical_not(jnp.logical_and(layer == me.z, core == me.core)))
-            def _():
-                signal(barrier, me.device(core=core, z=layer))
-
-    for core in range(CORES):
-        signal(barrier, me.device(x=other_x, core=core))
+    def greet(index, _):
+        pipe, layer = index // layers, index % layers
+
+        @pl.when(jnp.logical_not(jnp.logical_and(pipe == me.pipe, layer == me.z)))
+        def _():
+            signal(barrier, {"pipe": pipe, "dp": layer * CORES + me.y})
+
+        return 0
+
+    lax.fori_loop(0, layers * layers, greet, 0)
     signal(barrier, me.device(y=other_y))
-
-    @pl.when(jnp.logical_not(at_home))
-    def _():
-        signal(barrier, {"pipe": me.z, "dp": me.pipe * CORES + me.y})
-
-    pl.semaphore_wait(barrier, layers * CORES + 2 + jnp.where(at_home, 0, 1))
-
-    swap = {"pipe": me.z, "dp": me.pipe * CORES + me.y}
+    pl.semaphore_wait(barrier, layers * layers)
+
+    away = {"pipe": turned(me.z), "dp": me.pipe * CORES + me.y}
+    back = {"pipe": me.z, "dp": turned(me.pipe) * CORES + me.y}
+    stays = jnp.logical_and(at_home, turned(me.pipe) == me.pipe)
     swaps = ((input_ref, work_in), (home_mask_ref, mask))
 
     def swap_far(index):
         src, dst = swaps[index]
-        return remote(src, dst, swap_send.at[index], swap_recv.at[index], swap)
+        return remote(src, dst, swap_send.at[index], swap_recv.at[index], away)
 
     def swap_near(index):
         src, dst = swaps[index]
@@ -559,7 +563,7 @@
 
     def swap_start():
         for index in range(2):
-            either(at_home, lambda: swap_near(index).start(), lambda: swap_far(index).start())
+            either(stays, lambda: swap_near(index).start(), lambda: swap_far(index).start())
 
     def before(which, core):
         return remote(
@@ -615,8 +619,9 @@
 
     top_far = remote(top_ref, top, top_send, top_recv, me.device(z=layers - 1))
     top_near = pltpu.make_async_copy(top_ref, top, top_recv)
-    gives_top = jnp.logical_and(at_home, me.pipe < layers - 1)
-    keeps_top = jnp.logical_and(at_home, me.pipe == layers - 1)
+    has_top = me.z == turned(me.pipe)
+    gives_top = jnp.logical_and(has_top, jnp.logical_not(is_last))
+    keeps_top = jnp.logical_and(has_top, is_last)
 
     def top_start():
         pl.when(gives_top)(lambda: top_far.start())
@@ -657,56 +662,61 @@
             near = other_x * CORES + source == me.z
             pl.when(jnp.logical_not(near))(lambda: hop(which, source).wait_send())
 
-    for step in range(layers + 2):
+    def direct_ready(which, step):
+        block = direct_block(step)
+        if step == 0:
+            far = jnp.logical_and(me.x == me.z // CORES, me.core != me.z % CORES)
+            place = quarter(which, block, me.x, me.core)
+            either(
+                jnp.logical_not(far),
+                lambda: pltpu.make_async_copy(shard(which, 0, 0), place, came_at(which, block, me.x, me.core)).wait(),
+                lambda: arrived(which, block, me.x, me.core).wait_recv(),
+            )
+        else:
+            arrived(which, block, me.x, me.core).wait_recv()
+        x_copy(which, step).start()
+        y_copy(which, 0, step).start()
+        core_copy(which, 0, step).start()
+
+    def from_x(which, step):
+        arrived(which, direct_block(step), other_x, me.core).wait_recv()
+        y_copy(which, 1, step).start()
+        core_copy(which, 1, step).start()
+
+    def from_y(which, kind, step):
+        block = direct_block(step) - me.y + other_y
+        arrived(which, block, me.x if kind == 0 else other_x, me.core).wait_recv()
+        core_copy(which, 2 + kind, step).start()
+
+    def whole(which):
+        def one(index, _):
+            arrived(which, index // 2, index % 2, other_core).wait_recv()
+            return 0
+
+        lax.fori_loop(0, 2 * layers * CORES, one, 0)
+
+    for step in range(layers + 1):
         if step == 2:
             for which in range(2):
                 settled(which)
             swap_start()
             top_start()
-        for which in range(2):
-            if step < layers:
-                block = direct_block(step)
-                if step == 0:
-                    far = jnp.logical_and(me.x == me.z // CORES, me.core != me.z % CORES)
-                    place = quarter(which, block, me.x, me.core)
-                    either(
-                        jnp.logical_not(far),
-                        lambda: pltpu.make_async_copy(
-                            shard(which, 0, 0), place, came_at(which, block, me.x, me.core)
-                        ).wait(),
-                        lambda: arrived(which, block, me.x, me.core).wait_recv(),
-                    )
-                else:
-                    arrived(which, block, me.x, me.core).wait_recv()
-                x_copy(which, step).start()
-                y_copy(which, 0, step).start()
-                core_copy(which, 0, step).start()
-        for which in range(2):
-            if 1 <= step <= layers:
-                block = direct_block(step - 1)
-                arrived(which, block, other_x, me.core).wait_recv()
-                y_copy(which, 1, step - 1).start()
-                core_copy(which, 1, step - 1).start()
-                arrived(which, block - me.y + other_y, me.x, me.core).wait_recv()
-                core_copy(which, 2, step - 1).start()
-        for which in range(2):
-            if step >= 2:
-                block = direct_block(step - 2)
-                arrived(which, block - me.y + other_y, other_x, me.core).wait_recv()
-                core_copy(which, 3, step - 2).start()
-
+        if step < layers:
+            direct_ready(0, step)
+        if step >= 1:
+            from_x(0, step - 1)
+            from_y(0, 0, step - 1)
+        if step >= 2:
+            from_y(0, 1, step - 2)
+    for step in range(layers):
+        direct_ready(1, step)
     for index in range(2):
-        either(at_home, lambda: swap_near(index).wait(), lambda: swap_far(index).wait_recv())
-
-    for which in range(2):
-        def landed_all(index, _):
-            block, half = index // 2, index % 2
-            arrived(which, block, half, other_core).wait_recv()
-            return 0
-
-        lax.fori_loop(0, 2 * layers * CORES, landed_all, 0)
-
+        either(stays, lambda: swap_near(index).wait(), lambda: swap_far(index).wait_recv())
     norm_input(work_in, normed_ref, unit_in, rstd_in)
+    from_y(0, 1, layers - 1)
+    for step in range(layers):
+        from_x(1, step)
+    whole(0)
     tile = 2 * LANES
 
     def front(index, _):
@@ -718,7 +728,12 @@
         return 0
 
     lax.fori_loop(0, slope.shape[1] // tile, front, 0)
+    for step in range(layers):
+        from_y(1, 0, step)
     attend_front(micro, length, act, mask, weight, weight_slope, unit, rstd, gated_ref, mixed)
+    for step in range(layers):
+        from_y(1, 1, step)
+    whole(1)
 
     def copy_of(slot):
         return remote(
@@ -726,7 +741,22 @@
             me.device(z=jnp.maximum(me.z - 1, 0)),
         )
 
-    @pl.when(jnp.logical_and(is_last, jnp.logical_not(at_home)))
+    def back_far(slot):
+        rows = pl.ds(slot * length, length)
+        return remote(grads_ref.at[rows, :], out_grads.at[rows, :], back_send.at[slot], back_recv.at[slot], back)
+
+    def back_near(slot):
+        rows = pl.ds(slot * length, length)
+        return pltpu.make_async_copy(grads_ref.at[rows, :], out_grads.at[rows, :], back_recv.at[slot])
+
+    def back_one(slot):
+        either(stays, lambda: back_near(slot).start(), lambda: back_far(slot).start())
+
+    def back_start():
+        for slot in range(micro):
+            back_one(slot)
+
+    @pl.when(jnp.logical_and(is_last, jnp.logical_not(has_top)))
     def _():
         top_far.wait_recv()
 
@@ -735,7 +765,7 @@
         top_near.wait()
 
     chain_steps(
-        micro, length, is_first, is_last, copy_of,
+        micro, length, is_first, is_last, copy_of, back_one,
         top, unit_in, rstd_in, act, slope, weight, weight_slope, unit, rstd, first, second,
         grads_ref, up_ref, gpre_ref, landed, ggate, gnorm,
     )
@@ -747,7 +777,7 @@
             copy_of(slot).wait_send()
 
     for index in range(2):
-        pl.when(jnp.logical_not(at_home))(lambda: swap_far(index).wait_send())
+        pl.when(jnp.logical_not(stays))(lambda: swap_far(index).wait_send())
     pl.when(gives_top)(lambda: top_far.wait_send())
     for which in range(2):
         for core in range(CORES):
@@ -762,6 +792,13 @@
             return 0
 
         lax.fori_loop(0, layers, sent, 0)
+
+    sum_weights(
+        me, layers, normed_ref, gpre_ref, gated_ref, up_ref, out_first, out_second, first, second, *sums,
+        lambda: pl.when(jnp.logical_not(is_first))(back_start),
+    )
+    for slot in range(micro):
+        either(stays, lambda: back_near(slot).wait(), lambda: back_far(slot).wait())
 
 
 def folded(value):
@@ -832,7 +869,7 @@
 
 
 def chain_steps(
-    micro, length, is_first, is_last, copy_of,
+    micro, length, is_first, is_last, copy_of, back_one,
     top_ref, unit_in, rstd_in, act_ref, slope_ref, weight_ref, weight_slope, unit_ref, rstd_ref, first_ref, second_ref,
     grads_ref, up_ref, gpre_ref, landed, ggate, gnorm,
 ):
@@ -918,6 +955,8 @@
         def _():
             copy_of(slot).start()
 
+        back_one(slot)
+
 
 ANY = pl.BlockSpec(memory_space=pl.ANY)
 LIMIT = 60 * 1024 * 1024
@@ -931,16 +970,15 @@
     dma = pltpu.SemaphoreType.DMA
     return pl.pallas_call(
         functools.partial(work_kernel, micro, length, layers),
-        out_shape=(
-            jax.ShapeDtypeStruct((tokens, width), jnp.bfloat16),
-            jax.ShapeDtypeStruct((tokens, width), jnp.bfloat16),
-            jax.ShapeDtypeStruct((tokens, columns), jnp.bfloat16),
-            jax.ShapeDtypeStruct((tokens, width), jnp.bfloat16),
-            jax.ShapeDtypeStruct((tokens, V_COLS), jnp.bfloat16),
-        ),
+        out_shape=tuple(jax.ShapeDtypeStruct(a.shape, a.dtype) for a in (w_in, w_out, inputs)),
         in_specs=[ANY] * 5,
-        out_specs=(VMEM,) * 5,
+        out_specs=(ANY,) * 3,
         scratch_shapes=[
+            pltpu.VMEM((tokens, width), jnp.bfloat16),
+            pltpu.VMEM((tokens, width), jnp.bfloat16),
+            pltpu.VMEM((tokens, columns), jnp.bfloat16),
+            pltpu.VMEM((tokens, width), jnp.bfloat16),
+            pltpu.VMEM((tokens, V_COLS), jnp.bfloat16),
             pltpu.VMEM((blocks * w_in.shape[0], columns), jnp.bfloat16),
             pltpu.VMEM((blocks * w_out.shape[0], width), jnp.bfloat16),
             pltpu.VMEM((CORES, quarters[0], columns), jnp.bfloat16),
@@ -963,8 +1001,14 @@
             dma((2,)), dma((2,)), dma, dma,
             dma((2, CORES)), dma((2, CORES)), dma((2, CORES)), dma((2, CORES)),
             dma((2, 4 * layers)), dma((2, layers)), dma((2, 2 * layers)), dma((2, 4 * blocks)),
-            dma((micro,)), dma((micro,)),
-        ],
+            dma((micro,)), dma((micro,)), dma((micro,)), dma((micro,)),
+        ]
+        + [
+            pltpu.VMEM((count, size, cols), jnp.bfloat16)
+            for count in (2 * blocks, 2 * layers, layers)
+            for size, cols in zip(quarters, (columns, width))
+        ]
+        + [dma((2, count)) for count in (2 * blocks, 2 * layers, layers, layers) for _ in range(2)],
         compiler_params=pltpu.CompilerParams(collective_id=2, has_side_effects=True, vmem_limit_bytes=LIMIT),
         name="work",
     )(inputs, top_grad, w_in, w_out, mask)
@@ -982,38 +1026,19 @@
     lax.fori_loop(0, target.shape[0] // step, one, 0)
 
 
-def weight_kernel(
-    layers,
-    normed_ref, gpre_ref, gated_ref, up_ref, done_ref,
-    out_first, out_second, grads_ref,
-    first, second, core_first, core_second, y_first, y_second, x_first, x_second,
+def sum_weights(
+    me, layers, normed_ref, gpre_ref, gated_ref, up_ref, out_first, out_second, first, second,
+    core_first, core_second, early_first, early_second, late_first, late_second,
     core_send, core_recv, y_send, y_recv, x_send, x_recv, home_send, home_recv,
-    back_send, back_recv,
+    between,
 ):
-    me = Place()
     other_x, other_core, other_y = 1 - me.x, 1 - me.core, 1 - me.y
     at_home = me.pipe == me.z
     sets = (
-        (normed_ref, gpre_ref, out_first, first, core_first, y_first, x_first),
-        (gated_ref, up_ref, out_second, second, core_second, y_second, x_second),
+        (normed_ref, gpre_ref, out_first, first, core_first, early_first, late_first),
+        (gated_ref, up_ref, out_second, second, core_second, early_second, late_second),
     )
     sizes = [s[2].shape[0] // 4 for s in sets]
-
-    barrier = pltpu.get_barrier_semaphore()
-    signal(barrier, me.device(core=other_core))
-    signal(barrier, me.device(x=other_x))
-    signal(barrier, me.device(y=other_y))
-    for pipe in range(layers):
-
-        @pl.when(jnp.logical_not(jnp.logical_and(at_home, pipe == me.pipe)))
-        def _():
-            signal(barrier, {"pipe": pipe, "dp": me.pipe * CORES + me.y})
-
-    pl.semaphore_wait(barrier, 3 + layers - jnp.where(at_home, 1, 0))
-
-    back_far = remote(done_ref, grads_ref, back_send, back_recv, {"pipe": me.z, "dp": me.pipe * CORES + me.y})
-    back_near = pltpu.make_async_copy(done_ref, grads_ref, back_recv)
-    either(at_home, lambda: back_near.start(), lambda: back_far.start())
 
     def quarter(which, block, half, core):
         size = sizes[which]
@@ -1028,19 +1053,34 @@
             core_send.at[which, index], core_recv.at[which, index], me.device(core=other_core),
         )
 
-    def y_copy(which, row, half, mine):
-        block = row * CORES + (me.y if mine else other_y)
-        index = row * 2 + half
+    along_y = me.core == 0
+    early_to = {
+        "pipe": jnp.where(along_y, me.x, other_x) * CORES + me.core,
+        "dp": me.z * CORES + jnp.where(along_y, other_y, me.y),
+    }
+    late_to = {
+        "pipe": jnp.where(along_y, other_x, me.x) * CORES + me.core,
+        "dp": me.z * CORES + jnp.where(along_y, me.y, other_y),
+    }
+
+    def near_unit(row, index, far):
+        lane_of = jnp.where(along_y, other_y if far else me.y, index)
+        half = jnp.where(along_y, index, other_x if far else me.x)
+        return row * CORES + lane_of, half
+
+    def early_copy(which, row, index):
+        block, half = near_unit(row, index, True)
+        slot = row * 2 + index
         return remote(
-            quarter(which, block, half, me.core), sets[which][5].at[index],
-            y_send.at[which, index], y_recv.at[which, index], me.device(y=other_y),
-        )
-
-    def x_copy(which, row, mine):
-        block = row * CORES + me.y
+            quarter(which, block, half, me.core), sets[which][5].at[slot],
+            y_send.at[which, slot], y_recv.at[which, slot], early_to,
+        )
+
+    def late_copy(which, row):
+        block, half = near_unit(row, jnp.where(along_y, other_x, other_y), False)
         return remote(
-            quarter(which, block, me.x if mine else other_x, me.core), sets[which][6].at[row],
-            x_send.at[which, row], x_recv.at[which, row], me.device(x=other_x),
+            quarter(which, block, half, me.core), sets[which][6].at[row],
+            x_send.at[which, row], x_recv.at[which, row], late_to,
         )
 
     def home_rows(which, half, core):
@@ -1063,13 +1103,12 @@
     def row_at(step):
         return layer_order(layers - 1 - step, me.z, layers)
 
-    def product(which, row):
-        left, right, _, whole = sets[which][:4]
-        size = 4 * sizes[which]
-        tile = 2 * LANES
-        for lane_of in (other_y, me.y):
-            block = row * CORES + lane_of
-            place = pl.ds(pl.multiple_of(block * size, size), size)
+    def product(row):
+        for which in (1, 0):
+            left, right, _, whole = sets[which][:4]
+            size = 8 * sizes[which]
+            tile = 2 * LANES
+            place = pl.ds(pl.multiple_of(row * size, size), size)
 
             def one(index, _):
                 cols = at(index * tile, tile)
@@ -1077,59 +1116,67 @@
                 return 0
 
             lax.fori_loop(0, right.shape[1] // tile, one, 0)
-            for half in range(2):
-                core_copy(which, block, half, False).start()
-
-    def fold_y(which, row):
-        for half in range(2):
-            block = row * CORES + other_y
-            core_copy(which, block, half, True).wait_recv()
-            add_rows(quarter(which, block, half, me.core), sets[which][4].at[block * 2 + half])
-            y_copy(which, row, half, False).start()
-
-    def fold_x(which, row):
-        for half in (other_x, me.x):
-            block = row * CORES + me.y
-            core_copy(which, block, half, True).wait_recv()
-            place = quarter(which, block, half, me.core)
-            add_rows(place, sets[which][4].at[block * 2 + half])
-            y_copy(which, row, half, True).wait_recv()
-            add_rows(place, sets[which][5].at[row * 2 + half])
-
-            @pl.when(half == other_x)
-            def _():
-                x_copy(which, row, False).start()
-
-    def fold_home(which, row):
-        x_copy(which, row, True).wait_recv()
-        add_rows(quarter(which, row * CORES + me.y, me.x, me.core), sets[which][6].at[row])
-        near = jnp.logical_and(at_home, row == me.z)
-        either(near, lambda: home_near(which).start(), lambda: home_copy(which, row).start())
-
-    def run(step, _):
-        for which in range(2):
-
-            @pl.when(step < layers)
-            def _():
-                product(which, row_at(step))
-
-            @pl.when(jnp.logical_and(step >= 1, step < layers + 1))
-            def _():
-                fold_y(which, row_at(step - 1))
-
-            @pl.when(jnp.logical_and(step >= 2, step < layers + 2))
-            def _():
-                fold_x(which, row_at(step - 2))
-
-            @pl.when(step >= 3)
-            def _():
-                fold_home(which, row_at(step - 3))
-
-        return 0
-
-    lax.fori_loop(0, layers + 3, run, 0)
-    either(at_home, lambda: back_near.wait(), lambda: back_far.wait())
-
+            for lane_of in range(CORES):
+                for half in range(2):
+                    core_copy(which, row * CORES + lane_of, half, False).start()
+
+    def fold_core(row, far):
+        for which in (1, 0):
+
+            def one(index, _):
+                block, half = near_unit(row, index, far)
+                core_copy(which, block, half, True).wait_recv()
+                add_rows(quarter(which, block, half, me.core), sets[which][4].at[block * 2 + half])
+                return 0
+
+            lax.fori_loop(0, 2, one, 0)
+
+    def start_early(row):
+        for which in (1, 0):
+            for index in range(2):
+                early_copy(which, row, index).start()
+
+    def fold_early(row):
+        for which in (1, 0):
+
+            def one(turn, _):
+                mine = jnp.where(along_y, me.x, me.y)
+                index = jnp.where(turn == 0, 1 - mine, mine)
+                block, half = near_unit(row, index, False)
+                early_copy(which, row, index).wait_recv()
+                add_rows(quarter(which, block, half, me.core), sets[which][5].at[row * 2 + index])
+                pl.when(turn == 0)(lambda: late_copy(which, row).start())
+                return 0
+
+            lax.fori_loop(0, 2, one, 0)
+
+    def fold_late(row):
+        for which in (1, 0):
+            late_copy(which, row).wait_recv()
+            add_rows(quarter(which, row * CORES + me.y, me.x, me.core), sets[which][6].at[row])
+            near = jnp.logical_and(at_home, row == me.z)
+            either(near, lambda: home_near(which).start(), lambda: home_copy(which, row).start())
+
+    steps = [row_at(step) for step in range(layers)]
+    ahead = 1
+    for step in range(layers + 1):
+        if step < layers:
+            product(steps[step])
+        if step >= 1:
+            fold_core(steps[step - 1], True)
+            if step <= ahead:
+                start_early(steps[step - 1])
+            fold_core(steps[step - 1], False)
+    for step in range(layers + 1):
+        if step < layers:
+            if step + ahead < layers:
+                for which in (1, 0):
+                    early_copy(which, steps[step], 0).wait_send()
+                    early_copy(which, steps[step], 1).wait_send()
+                start_early(steps[step + ahead])
+            fold_early(steps[step])
+        if step >= 1:
+            fold_late(steps[step - 1])
     for which in range(2):
         for pipe in range(layers):
             place = home_rows(which, pipe // CORES, pipe % CORES)
@@ -1146,46 +1193,22 @@
             for half in range(2):
                 for lane_of in range(2):
                     core_copy(which, row * CORES + lane_of, half, False).wait_send()
-                y_copy(which, row, half, False).wait_send()
-            x_copy(which, row, False).wait_send()
             near = jnp.logical_and(at_home, row == me.z)
             pl.when(jnp.logical_not(near))(lambda: home_copy(which, row).wait_send())
             return 0
 
         lax.fori_loop(0, layers, sent, 0)
-
-
-def weight_sums(normed, grad_preact, gated, upstream, grads):
-    layers, blocks = lax.axis_size("pipe"), lax.axis_size("dp")
-    dma = pltpu.SemaphoreType.DMA
-    pairs = ((normed, grad_preact), (gated, upstream))
-    shapes = [(left.shape[1], right.shape[1]) for left, right in pairs]
-    scratch = [pltpu.VMEM(shape, jnp.bfloat16) for shape in shapes]
-    for count in (2 * blocks, 2 * layers, layers):
-        for rows, cols in shapes:
-            scratch.append(pltpu.VMEM((count, rows // (4 * blocks), cols), jnp.bfloat16))
-    for count in (2 * blocks, 2 * layers, layers, layers):
-        scratch += [dma((2, count))] * 2
-    scratch += [dma, dma]
-    return pl.pallas_call(
-        functools.partial(weight_kernel, layers),
-        out_shape=tuple(jax.ShapeDtypeStruct((rows // blocks, cols), jnp.bfloat16) for rows, cols in shapes)
-        + (jax.ShapeDtypeStruct(grads.shape, grads.dtype),),
-        in_specs=[VMEM] * 4 + [ANY],
-        out_specs=(ANY,) * 3,
-        scratch_shapes=scratch,
-        compiler_params=pltpu.CompilerParams(collective_id=3, has_side_effects=True, vmem_limit_bytes=LIMIT),
-        name="weight_sums",
-    )(normed, grad_preact, gated, upstream, grads)
+        for step in range(layers):
+            if step + ahead >= layers:
+                early_copy(which, steps[step], 0).wait_send()
+                early_copy(which, steps[step], 1).wait_send()
+            late_copy(which, steps[step]).wait_send()
 
 
 def layered_body(section_input, top_grad, w_in, w_out, segments):
     micro, length = segments.shape
     mask = mask_of(segments)
-    grads, upstream, grad_preact, normed, gated = work(
-        section_input[0], top_grad, w_in[0], w_out[0], mask, micro, length
-    )
-    grad_first, grad_out, grads = weight_sums(normed, grad_preact, gated, upstream, grads)
+    grad_first, grad_out, grads = work(section_input[0], top_grad, w_in[0], w_out[0], mask, micro, length)
     return (grads[None], grad_first.astype(jnp.float32)[None], grad_out.astype(jnp.float32)[None])
 
 

time: 380 us -> 357 us (0.939)
  the two profiles are of different devices: /device:TPU:22 before, /device:TPU:4 now
where the time goes in v3:
time: 357 us
  Pallas kernels  348 us (97%)
  other arithmetic  7.07 us (2%)
    pallas_call x1, Pallas kernels, work(): pl.pallas_call(functools.partial(work_kernel, micro, length, layers), out...  348 us

profile of v3, /device:TPU:4, one launch (start us, length us, event | category | flops | bytes accessed | tf_op | source)
XLA Modules:
  0.0 356.9 jit_solution(6673472295896240350)
XLA Ops:
  0.7 0.9 convert_reduce_fusion
  1.6 1.6 convert_divide_fusion.home_mask_ref
  3.1 347.7 %work.1 = (bf16[256,3072]{1,0:T(8,128)(2,1)}, bf16[128,2048]{1,0:T(8,128)(2,1)}, bf16[256,2048]{1,0:T(8,128)(2,1)}) custom-call(bf16[256,2048]{1,0:T(8,128)(2,1)} %bitcast.22, bf16[256,2048]{1,0:T(8,128)(2,1)} %top_ref.1, bf16[256,3072]{1,0:T(8,128)(2,1)} %bitcast.20, bf16[128,2048]{1,0:T(8,128)(2,1)} %bitcast.23, f32[256,128]{1,0:T(8,128)} %convert_divide_fusion.home_mask_ref), custom_call_target="tpu_custom_call" | custom-call | tf_op jit(solution)/shard_map/work/pallas_call | solution.py:971
  350.9 0.0 copy-start.1
  350.9 3.5 bitcast_convert_fusion
  354.4 0.0 copy-start
  354.4 0.0 copy-done.1
  354.4 1.1 bitcast_convert_fusion.1
  355.4 0.5 copy-done
  356.0 1.0 copy.9
  (1 shorter events, 0.0 us)
Async XLA Ops:
  350.9 3.5 copy-start.1
  354.4 1.6 copy-start

commit v4 on v3

--- a/solution.py
+++ b/solution.py
@@ -696,7 +696,7 @@
         lax.fori_loop(0, 2 * layers * CORES, one, 0)
 
     for step in range(layers + 1):
-        if step == 2:
+        if step == 3:
             for which in range(2):
                 settled(which)
             swap_start()
@@ -1158,7 +1158,7 @@
             either(near, lambda: home_near(which).start(), lambda: home_copy(which, row).start())
 
     steps = [row_at(step) for step in range(layers)]
-    ahead = 1
+    ahead = 2
     for step in range(layers + 1):
         if step < layers:
             product(steps[step])

time: 357 us -> 350 us (0.980)
  Pallas kernels: 348 us -> 341 us
    pallas_call x1, Pallas kernels: 348 us -> 341 us  [work(): pl.pallas_call(functools.partial(work_kernel, micro, length, layers), out...]
where the time goes in v4:
time: 350 us
  Pallas kernels  341 us (97%)
  other arithmetic  7.07 us (2%)
    pallas_call x1, Pallas kernels, work(): pl.pallas_call(functools.partial(work_kernel, micro, length, layers), out...  341 us

profile of v4, /device:TPU:4, one launch (start us, length us, event | category | flops | bytes accessed | tf_op | source)
XLA Modules:
  0.0 349.9 jit_solution(13222137017481400157)
XLA Ops:
  0.7 0.9 convert_reduce_fusion
  1.6 1.6 convert_divide_fusion.home_mask_ref
  3.1 340.7 %work.1 = (bf16[256,3072]{1,0:T(8,128)(2,1)}, bf16[128,2048]{1,0:T(8,128)(2,1)}, bf16[256,2048]{1,0:T(8,128)(2,1)}) custom-call(bf16[256,2048]{1,0:T(8,128)(2,1)} %bitcast.22, bf16[256,2048]{1,0:T(8,128)(2,1)} %top_ref.1, bf16[256,3072]{1,0:T(8,128)(2,1)} %bitcast.20, bf16[128,2048]{1,0:T(8,128)(2,1)} %bitcast.23, f32[256,128]{1,0:T(8,128)} %convert_divide_fusion.home_mask_ref), custom_call_target="tpu_custom_call" | custom-call | tf_op jit(solution)/shard_map/work/pallas_call | solution.py:971
  343.8 0.0 copy-start.1
  343.8 3.5 bitcast_convert_fusion
  347.3 0.0 copy-start
  347.3 0.0 copy-done.1
  347.3 1.1 bitcast_convert_fusion.1
  348.4 0.5 copy-done
  348.9 1.0 copy.9
  (1 shorter events, 0.0 us)
Async XLA Ops:
  343.8 3.5 %copy-start.1 = (bf16[128,2048]{1,0:T(8,128)(2,1)S(1)}, bf16[128,2048]{1,0:T(8,128)(2,1)}, u32[]{:S(2)}) copy-start(bf16[128,2048]{1,0:T(8,128)(2,1)} %get-tuple-element.8) | copy-start | bytes 1572868
  347.3 1.6 copy-start

commit v5 on v4

--- a/solution.py
+++ b/solution.py
@@ -700,7 +700,6 @@
             for which in range(2):
                 settled(which)
             swap_start()
-            top_start()
         if step < layers:
             direct_ready(0, step)
         if step >= 1:
@@ -708,6 +707,7 @@
             from_y(0, 0, step - 1)
         if step >= 2:
             from_y(0, 1, step - 2)
+    top_start()
     for step in range(layers):
         direct_ready(1, step)
     for index in range(2):

time: 350 us -> 341 us (0.974)
  Pallas kernels: 341 us -> 332 us
    pallas_call x1, Pallas kernels: 341 us -> 332 us  [work(): pl.pallas_call(functools.partial(work_kernel, micro, length, layers), out...]
where the time goes in v5:
time: 341 us
  Pallas kernels  332 us (97%)
  other arithmetic  7.07 us (2%)
    pallas_call x1, Pallas kernels, work(): pl.pallas_call(functools.partial(work_kernel, micro, length, layers), out...  332 us

profile of v5, /device:TPU:4, one launch (start us, length us, event | category | flops | bytes accessed | tf_op | source)
XLA Modules:
  0.0 341.1 jit_solution(4260540570469916027)
XLA Ops:
  0.7 0.9 convert_reduce_fusion
  1.6 1.6 convert_divide_fusion.home_mask_ref
  3.1 331.8 %work.1 = (bf16[256,3072]{1,0:T(8,128)(2,1)}, bf16[128,2048]{1,0:T(8,128)(2,1)}, bf16[256,2048]{1,0:T(8,128)(2,1)}) custom-call(bf16[256,2048]{1,0:T(8,128)(2,1)} %bitcast.22, bf16[256,2048]{1,0:T(8,128)(2,1)} %top_ref.1, bf16[256,3072]{1,0:T(8,128)(2,1)} %bitcast.20, bf16[128,2048]{1,0:T(8,128)(2,1)} %bitcast.23, f32[256,128]{1,0:T(8,128)} %convert_divide_fusion.home_mask_ref), custom_call_target="tpu_custom_call" | custom-call | tf_op jit(solution)/shard_map/work/pallas_call | solution.py:971
  335.0 0.0 copy-start.1
  335.0 3.5 %bitcast_convert_fusion = f32[1,256,3072]{2,1,0:T(8,128)} fusion(bf16[256,3072]{1,0:T(8,128)(2,1)} %get-tuple-element.7), kind=kLoop, calls=%fused_computation | loop fusion | flops 786432 | bytes 4718592 | tf_op jit(solution)/shard_map/broadcast_in_dim | solution.py:1212
  338.5 0.0 copy-start
  338.5 0.0 copy-done.1
  338.5 1.1 bitcast_convert_fusion.1
  339.6 0.5 copy-done
  340.1 1.0 copy.9
  (1 shorter events, 0.0 us)
Async XLA Ops:
  335.0 3.5 %copy-start.1 = (bf16[128,2048]{1,0:T(8,128)(2,1)S(1)}, bf16[128,2048]{1,0:T(8,128)(2,1)}, u32[]{:S(2)}) copy-start(bf16[128,2048]{1,0:T(8,128)(2,1)} %get-tuple-element.8) | copy-start | bytes 1572868
  338.5 1.6 copy-start
